TPU v7x, 768 devices: a whole 4x8x12 slice. The times are simulated.
768 devices in a mesh: lon: 64 (over x, y, core), lat: 12 (over z).
Axes of the slice: x: 4, y: 8, z: 12, core: 2. Of those that a mesh axis runs over, the one named last changes fastest.
Arguments:
- state_prev: float32 [7, 16, 192, 8192], P(None, None, 'lat', 'lon'), may hold values from -6 to 6
- state_now: float32 [7, 16, 192, 8192], P(None, None, 'lat', 'lon'), may hold values from -6 to 6
- stride_table: int32 [192], P('lat'), may hold values from 1 to 32, as said below
- filter_len: int32 [192], P('lat'), may hold values from 1 to 32, as said below
- zonal_coef: float32 [192], P('lat'), may hold values from 0.05 to 0.3
- merid_coef: float32 [16], replicated, may hold values from 0.05 to 0.3
- filter_coef: float32 [16], replicated, may hold values from 0.03 to 0.2
- w_first: bfloat16 [7, 64], replicated, may hold values from -2 to 2
- b_first: float32 [64], replicated, may hold values from -3 to 3
- w_second: bfloat16 [64, 64], replicated, may hold values from -0.75 to 0.75
- b_second: float32 [64], replicated, may hold values from -3 to 3
- w_third: bfloat16 [64, 224], replicated, may hold values from -0.75 to 0.75
- b_third: float32 [224], replicated, may hold values from -3 to 3
- band_weight: float32 [224], replicated, may hold values from 0.02 to 0.2
- sunlit_cols: int32 [12, 64, 1536], P('lat', 'lon'), may hold values from 0 to 2047, as said below
- sunlit_count: int32 [12, 64], P('lat'), may hold values from 0 to 1536, as said below
Outputs:
- prev_out: float32 [7, 16, 192, 8192], P(None, None, 'lat', 'lon')
- now_out: float32 [7, 16, 192, 8192], P(None, None, 'lat', 'lon')
Inputs may be any that keep to these rules, and one draw needn't show every extreme that they name: `stride_table`: 1 except in the 4 rows nearest each end of the latitude range. `filter_len`: 1 except in the 4 rows nearest each end of the latitude range. `sunlit_cols`: the entries of one device's list are distinct. `sunlit_count`: a device's count plus that of the device 64 / 2 further along lon (cyclic) in the same band is at most 1536.
All inputs are finite; a program needn't handle non-finite values.
Results may differ from a plain program's by a relative error of at most 0.0003.
Values may be sent and summed in bfloat16 or wider, within the bound.
No kernel may reach another device: no remote copies, remote signals or barrier semaphores. Data moves between devices by JAX's collectives and lax.ppermute only.
A program may use at most 64 MiB of HBM per device.

v0:
```python
import jax
import jax.numpy as jnp
from jax import lax
from jax.sharding import PartitionSpec as P

SMAX = 32
POLAR = 4
BLK = 128


def extended(cells, sides, width, closed):
    for axis, dim in sides:
        count = lax.axis_size(axis)
        ends = count if closed else count - 1
        head = lax.slice_in_dim(cells, 0, width, axis=dim)
        tail = lax.slice_in_dim(cells, cells.shape[dim] - width, cells.shape[dim], axis=dim)
        cells = jnp.concatenate(
            [
                lax.ppermute(tail, axis, [(i, (i + 1) % count) for i in range(ends)]),
                cells,
                lax.ppermute(head, axis, [((i + 1) % count, i) for i in range(ends)]),
            ],
            axis=dim,
        )
    return cells


def shifted_2(block, axis, distance):
    devices = range(lax.axis_size(axis))
    route = [((i - distance) % len(devices), i) for i in devices]
    return lax.ppermute(block, axis, route)


def absorb(feats_t, w_first, b_first, w_second, b_second, w_third, b_third, band_weight):
    count = feats_t.shape[2]
    levels = feats_t.shape[1]
    rows = jnp.transpose(feats_t, (2, 1, 0)).reshape(count * levels, feats_t.shape[0])
    first = jax.nn.silu(
        jnp.dot(rows, w_first, preferred_element_type=jnp.float32) + b_first
    ).astype(jnp.bfloat16)
    second = jax.nn.silu(
        jnp.dot(first, w_second, preferred_element_type=jnp.float32) + b_second
    ).astype(jnp.bfloat16)
    tau = 0.15 * jax.nn.softplus(
        jnp.dot(second, w_third, preferred_element_type=jnp.float32) + b_third
    )
    tau = tau.reshape(count, levels, tau.shape[-1])
    depth = jnp.cumsum(tau, axis=1)
    above = depth - tau
    return jnp.sum((jnp.exp(-above) - jnp.exp(-depth)) * band_weight, axis=-1)


def network(feats_t, weights):
    groups = feats_t.shape[2] // BLK
    blocks = jnp.moveaxis(feats_t.reshape(feats_t.shape[0], feats_t.shape[1], groups, BLK), 2, 0)
    heats = lax.map(lambda block: absorb(block, *weights), blocks)
    return heats.reshape(groups * BLK, feats_t.shape[1])


def shifted(center, offsets, sign, pstart, width):
    static = center[:, :, :, SMAX + sign : SMAX + sign + width]
    pieces = []
    for place in range(POLAR):
        row_at = pstart + place
        row = lax.dynamic_index_in_dim(center, row_at, 2, False)
        start = SMAX + sign * offsets[row_at]
        pieces.append(lax.dynamic_slice_in_dim(row, start, width, 2))
    slab = jnp.stack(pieces, axis=2)
    return lax.dynamic_update_slice_in_dim(static, slab, pstart, 2)


def tendency(center, merid, stride, flen, zcoef, merid_coef, filter_coef, pstart, width):
    field = center[:, :, :, SMAX : SMAX + width]
    inv_s = 1.0 / stride.astype(jnp.float32)
    plus = shifted(center, stride, 1, pstart, width)
    minus = shifted(center, stride, -1, pstart, width)
    fplus = shifted(center, flen, 1, pstart, width)
    fminus = shifted(center, flen, -1, pstart, width)
    wind_u = field[0][None]
    wind_v = field[1][None]
    tend = -zcoef[None, None, :, None] * wind_u * ((plus - minus) * inv_s[None, None, :, None])
    tend = tend - merid_coef[None, :, None, None] * wind_v * merid
    tend = tend + filter_coef[None, :, None, None] * (fplus - 2.0 * field + fminus)
    return tend


def polar_start(rows):
    return jnp.where(lax.axis_index("lat") == 0, 0, rows - POLAR).astype(jnp.int32)


def zonal_cells(now):
    return extended(now, (("lon", 3),), SMAX, True)


def leap(prev, now, stride_table, filter_len, zonal_coef, merid_coef, filter_coef):
    wide = zonal_cells(now)
    banded = extended(now, (("lat", 2),), 1, False)
    merid = banded[:, :, 2:] - banded[:, :, :-2]
    pstart = polar_start(now.shape[2])
    tend = tendency(
        wide,
        merid,
        stride_table,
        filter_len,
        zonal_coef,
        merid_coef,
        filter_coef,
        pstart,
        now.shape[3],
    )
    new = prev + tend
    return (now + 0.1 * (prev - 2.0 * now + new), new)


def body(
    state_prev,
    state_now,
    stride_table,
    filter_len,
    zonal_coef,
    merid_coef,
    filter_coef,
    w_first,
    b_first,
    w_second,
    b_second,
    w_third,
    b_third,
    band_weight,
    sunlit_cols,
    sunlit_count,
):
    prev, now = (state_prev, state_now)
    for turn in range(2):
        prev, now = leap(prev, now, stride_table, filter_len, zonal_coef, merid_coef, filter_coef)
    weights = (w_first, b_first, w_second, b_second, w_third, b_third, band_weight)
    cells = now.shape[2] * now.shape[3]
    flat = now.reshape(now.shape[0], now.shape[1], cells)
    listed = sunlit_cols.reshape(-1)
    slots_all = listed.shape[0]
    feats_t = jnp.take(flat, listed, axis=2).astype(jnp.bfloat16)
    lon_here = lax.axis_index("lon")
    lon_count = lax.axis_size("lon")
    counts_row = sunlit_count.reshape(-1)
    mine = counts_row[lon_here]
    half = slots_all // 2
    other = counts_row[(lon_here + lon_count // 2) % lon_count]
    excess = feats_t[:, :, half:]
    arrived = shifted_2(excess, "lon", lon_count // 2)
    slots = jnp.arange(half, dtype=jnp.int32)
    place = jnp.clip(slots - mine, 0, half - 1)
    buffer = jnp.where(
        (slots < mine)[None, None, :], feats_t[:, :, :half], jnp.take(arrived, place, axis=2)
    )
    computed = network(buffer, weights)
    over_other = jnp.maximum(other - half, 0)
    back_index = jnp.clip(mine + slots, 0, half - 1)
    outgoing = jnp.where((slots < over_other)[:, None], computed[back_index], jnp.float32(0.0))
    returned = shifted_2(outgoing.T, "lon", lon_count // 2)
    own = jnp.where((slots < mine)[:, None], computed, jnp.float32(0.0))
    heat = jnp.concatenate([own, returned.T], axis=0)
    temper = now[2].reshape(now.shape[1], cells).at[:, listed].add(heat.T)
    now_out = now.at[2].set(temper.reshape(now.shape[1], now.shape[2], now.shape[3]))
    return (prev, now_out)


def solution(mesh):
    in_specs = (
        P(None, None, "lat", "lon"),
        P(None, None, "lat", "lon"),
        P("lat"),
        P("lat"),
        P("lat"),
        P(),
        P(),
        P(),
        P(),
        P(),
        P(),
        P(),
        P(),
        P(),
        P("lat", "lon", None),
        P("lat", None),
    )
    out_specs = (P(None, None, "lat", "lon"), P(None, None, "lat", "lon"))
    return jax.shard_map(body, mesh=mesh, in_specs=in_specs, out_specs=out_specs, check_vma=False)
```

profile of v0, /device:TPU:192, one launch (start us, length us, event | category | flops | bytes accessed | tf_op | source)
XLA Modules:
  0.0 222.0 jit_solution(17779961135403854341)
XLA Ops:
  0.7 3.0 %fusion.32 = (f32[7,16,16,32]{3,2,1,0:T(8,128)}, f32[7,16,16,32]{3,2,1,0:T(8,128)}) fusion(f32[7,16,16,128]{3,2,1,0:T(8,128)} %param.21), kind=kLoop, calls=%fused_computation.119 | loop fusion | bytes 917504 | tf_op jit(solution)/shard_map/slice | solution.py:15
  3.8 7.0 %collective-permute-start = (f32[7,16,16,32]{3,2,1,0:T(8,128)}, f32[7,16,16,32]{3,2,1,0:T(8,128)S(1)}, u32[]{:S(2)}, u32[]{:S(2)}) collective-permute-start(f32[7,16,16,32]{3,2,1,0:T(8,128)} %get-tuple-element.163), channel_id=1, source_target_pairs={{12,0},{24,12},{36,24},{48,36},{60,48},{72,60},{84,72},{96,84},{10... | collective-permute-start | bytes 688136 | tf_op jit(solution)/shard_map/ppermute | solution.py:21
  12.8 1.9 collective-permute-start.2
  14.7 5.5 %collective-permute-start.3 = (f32[7,16,1,128]{3,2,1,0:T(1,128)S(1)}, f32[7,16,1,128]{3,2,1,0:T(1,128)S(1)}, u32[]{:S(2)}, u32[]{:S(2)}) collective-permute-start(f32[7,16,1,128]{3,2,1,0:T(1,128)S(1)} %get-tuple-element.166), channel_id=1, source_target_pairs={{0,1},{1,2},{2,3},{3,4},{4,5},{5,6},{6,7},{7,8},{8,9},{9,10},{10,1... | collective-permute-start | bytes 172040 | tf_op jit(solution)/shard_map/ppermute | solution.py:19
  42.7 2.6 %constant_dynamic-slice_fusion.29 = (f32[7,16,1,128]{3,2,1,0:T(1,128)S(1)}, f32[7,16,1,128]{3,2,1,0:T(1,128)S(1)}, f32[7,16,1,128]{3,2,1,0:T(1,128)S(1)}, f32[7,...) fusion(f32[7,16,16,192]{3,2,1,0:T(8,128)S(1)} %pad_maximum_fusi, ...), kind=kLoop, calls=%fused_computation.99 | loop fusion | bytes 1605704 | tf_op jit(solution)/shard_map/dynamic_slice | solution.py:67
  47.7 6.7 %collective-permute-start.4 = (f32[7,16,16,32]{3,2,1,0:T(8,128)S(1)}, f32[7,16,16,32]{3,2,1,0:T(8,128)S(1)}, u32[]{:S(2)}, u32[]{:S(2)}) collective-permute-start(f32[7,16,16,32]{3,2,1,0:T(8,128)S(1)} %get-tuple-element.157), channel_id=1, source_target_pairs={{12,0},{24,12},{36,24},{48,36},{60,48},{72,60},{84,72},{96,84},{10... | collective-permute-start | bytes 688136 | tf_op jit(solution)/shard_map/ppermute | solution.py:21
  58.2 5.3 %collective-permute-start.7 = (f32[7,16,1,128]{3,2,1,0:T(1,128)S(1)}, f32[7,16,1,128]{3,2,1,0:T(1,128)S(1)}, u32[]{:S(2)}, u32[]{:S(2)}) collective-permute-start(f32[7,16,1,128]{3,2,1,0:T(1,128)S(1)} %get-tuple-element.154), channel_id=1, source_target_pairs={{0,1},{1,2},{2,3},{3,4},{4,5},{5,6},{6,7},{7,8},{8,9},{9,10},{10,1... | collective-permute-start | bytes 172040 | tf_op jit(solution)/shard_map/ppermute | solution.py:19
  65.3 7.1 %collective-permute-done.5 = f32[7,16,16,32]{3,2,1,0:T(8,128)S(1)} collective-permute-done((f32[7,16,16,32]{3,2,1,0:T(8,128)S(1)}, f32[7,16,16,32]{3,2,1,0:T(8,128)S(1)}, u32[]{:S(2)}, u32[]{:S(2)}) %collective-permute-start.5) | collective-permute-done | bytes 229408 | tf_op jit(solution)/shard_map/ppermute | solution.py:19
  73.2 2.6 %constant_dynamic-slice_fusion.13 = (f32[7,16,1,128]{3,2,1,0:T(1,128)S(1)}, f32[7,16,1,128]{3,2,1,0:T(1,128)S(1)}, f32[7,16,1,128]{3,2,1,0:T(1,128)S(1)}, f32[7,...) fusion(f32[7,16,16,192]{3,2,1,0:T(8,128)S(1)} %pad_maximum_fusi, ...), kind=kLoop, calls=%fused_computation.83 | loop fusion | bytes 1605704 | tf_op jit(solution)/shard_map/dynamic_slice | solution.py:67
  80.4 4.0 %copy.54 = bf16[7,16,16,128]{1,0,3,2:T(8,128)(2,1)} copy(f32[7,16,16,128]{3,2,1,0:T(8,128)S(1)} %get-tuple-element.118) | data formatting | bytes 1376256 | tf_op jit(solution)/shard_map/add | solution.py:111
  84.3 6.0 %gather_fusion = bf16[1536,7,16]{2,1,0:T(8,128)(2,1)} fusion(bf16[7,16,2048]{1,0,2:T(8,128)(2,1)} %bitcast.93, s32[2048]{0:T(1024)S(1)} %pad_clamp_fusion), kind=kCustom, calls=%fused_computation | custom fusion | bytes 694272 | tf_op jit(solution)/shard_map/jit(_take)/gather | solution.py:141
  90.4 8.0 %fusion.6 = bf16[7,16,1536]{1,0,2:T(8,128)(2,1)S(1)} fusion(bf16[1536,7,16]{2,1,0:T(8,128)(2,1)} %gather_fusion, pred[1536]{0:T(1024)(128)(4,1)S(1)} %compare_and_fusion), kind=kLoop, calls=%fused_computation.20 | loop fusion | flops 172032 | bytes 689664 | tf_op jit(solution)/shard_map/convert_element_type | solution.py:141
  101.1 2.1 collective-permute-start.8
  105.5 4.3 %collective-permute-done.8 = bf16[7,16,768]{2,1,0:T(8,128)(2,1)S(1)} collective-permute-done((bf16[7,16,768]{2,1,0:T(8,128)(2,1)S(1)}, bf16[7,16,768]{2,1,0:T(8,128)(2,1)S(1)}, u32[]{:S(2)}, u32[]{:S(2)}) %collective-permute-start.8) | collective-permute-done | bytes 172064 | tf_op jit(solution)/shard_map/ppermute | solution.py:31
  110.9 3.2 %gather_fusion.1 = bf16[768,7,16]{2,1,0:T(8,128)(2,1)} fusion(bf16[7,16,768]{1,0,2:T(8,128)(2,1)S(1)} %copy.56, s32[1024]{0:T(1024)S(1)} %pad_clamp_fusion.2), kind=kCustom, calls=%fused_computation.1 | custom fusion | bytes 347136 | tf_op jit(solution)/shard_map/jit(_take)/gather | solution.py:153
  114.1 6.5 %slice_select_fusion = bf16[7,16,768]{1,0,2:T(8,128)(2,1)S(1)} fusion(bf16[7,16,1536]{1,0,2:T(8,128)(2,1)} %copy-done.1, bf16[768,7,16]{2,1,0:T(8,128)(2,1)} %gather_fusion.1, pred[768]{0:T(1024)(128)(4,1)S(1)} %get-tuple-element.182, pred[768]{0:T(1024)(128)(4,1)S(1)} %get-tuple-element.181), kind=kLoop, calls=%fused_computation.23 | loop fusion | flops 172032 | bytes 517632 | tf_op jit(solution)/shard_map/jit(_where)/select_n | solution.py:152
  121.4 77.9 %while.11 = (s32[]{:T(128)}, f32[6,128,16]{2,1,0:T(8,128)S(1)}, bf16[6,7,16,128]{2,3,1,0:T(8,128)(2,1)S(1)}, bf16[7,64]{1,0:T(8,128)(2,1)S(1)}, f32[64]{0:T(128)...) while((s32[]{:T(128)}, f32[6,128,16]{2,1,0:T(8,128)S(1)}, ...), condition=%wide.region_3.4_spmd, body=%wide.region_0.3_spmd.sunk | while | flops 92207104 | bytes 22424876 | solution.py:56
  122.5 2.7 %fusion.55 = f32[2048,224]{0,1:T(8,128)} fusion(bf16[64,224]{1,0:T(8,128)(2,1)S(1)} %get-tuple-element.273, f32[224]{0:T(256)S(1)} %get-tuple-element.274, bf16[2048,64]{0,1:T(8,128)(2,1)S(1)} %multiply_convert_fusion.3, bf16[64,64]{1,0:T(8,128)(2,1)S(1)} %get-tuple-element.271, f32[64]{0:T(128)S(1)} %get-tuple-element.272), kind=kOutput, calls=%fused_computation.10.clone.1 | convolution fusion | flops 79953920 | bytes 2135168 | tf_op jit(solution)/shard_map/while/body/eval_jaxpr/dot_general | solution.py:45
  131.5 2.8 %multiply_reduce_fusion.2 = f32[2048]{0:T(1024)S(1)} fusion(f32[2048,224]{0,1:T(8,128)} %copy.71, f32[2048,224]{0,1:T(8,128)} %fusion.55, f32[224]{0:T(256)S(1)} %get-tuple-element.275), kind=kLoop, calls=%fused_computation.11.clone.1 | loop fusion | flops 2750464 | bytes 3679104 | tf_op jit(solution)/shard_map/while/body/eval_jaxpr/reduce_sum | solution.py:50
  135.5 2.7 %fusion.55 = f32[2048,224]{0,1:T(8,128)} fusion(bf16[64,224]{1,0:T(8,128)(2,1)S(1)} %get-tuple-element.273, f32[224]{0:T(256)S(1)} %get-tuple-element.274, bf16[2048,64]{0,1:T(8,128)(2,1)S(1)} %multiply_convert_fusion.3, bf16[64,64]{1,0:T(8,128)(2,1)S(1)} %get-tuple-element.271, f32[64]{0:T(128)S(1)} %get-tuple-element.272), kind=kOutput, calls=%fused_computation.10.clone.1 | convolution fusion | flops 79953920 | bytes 2135168 | tf_op jit(solution)/shard_map/while/body/eval_jaxpr/dot_general | solution.py:45
  144.5 2.8 %multiply_reduce_fusion.2 = f32[2048]{0:T(1024)S(1)} fusion(f32[2048,224]{0,1:T(8,128)} %copy.71, f32[2048,224]{0,1:T(8,128)} %fusion.55, f32[224]{0:T(256)S(1)} %get-tuple-element.275), kind=kLoop, calls=%fused_computation.11.clone.1 | loop fusion | flops 2750464 | bytes 3679104 | tf_op jit(solution)/shard_map/while/body/eval_jaxpr/reduce_sum | solution.py:50
  148.5 2.7 %fusion.55 = f32[2048,224]{0,1:T(8,128)} fusion(bf16[64,224]{1,0:T(8,128)(2,1)S(1)} %get-tuple-element.273, f32[224]{0:T(256)S(1)} %get-tuple-element.274, bf16[2048,64]{0,1:T(8,128)(2,1)S(1)} %multiply_convert_fusion.3, bf16[64,64]{1,0:T(8,128)(2,1)S(1)} %get-tuple-element.271, f32[64]{0:T(128)S(1)} %get-tuple-element.272), kind=kOutput, calls=%fused_computation.10.clone.1 | convolution fusion | flops 79953920 | bytes 2135168 | tf_op jit(solution)/shard_map/while/body/eval_jaxpr/dot_general | solution.py:45
  157.5 2.8 %multiply_reduce_fusion.2 = f32[2048]{0:T(1024)S(1)} fusion(f32[2048,224]{0,1:T(8,128)} %copy.71, f32[2048,224]{0,1:T(8,128)} %fusion.55, f32[224]{0:T(256)S(1)} %get-tuple-element.275), kind=kLoop, calls=%fused_computation.11.clone.1 | loop fusion | flops 2750464 | bytes 3679104 | tf_op jit(solution)/shard_map/while/body/eval_jaxpr/reduce_sum | solution.py:50
  161.5 2.7 %fusion.55 = f32[2048,224]{0,1:T(8,128)} fusion(bf16[64,224]{1,0:T(8,128)(2,1)S(1)} %get-tuple-element.273, f32[224]{0:T(256)S(1)} %get-tuple-element.274, bf16[2048,64]{0,1:T(8,128)(2,1)S(1)} %multiply_convert_fusion.3, bf16[64,64]{1,0:T(8,128)(2,1)S(1)} %get-tuple-element.271, f32[64]{0:T(128)S(1)} %get-tuple-element.272), kind=kOutput, calls=%fused_computation.10.clone.1 | convolution fusion | flops 79953920 | bytes 2135168 | tf_op jit(solution)/shard_map/while/body/eval_jaxpr/dot_general | solution.py:45
  170.5 2.8 %multiply_reduce_fusion.2 = f32[2048]{0:T(1024)S(1)} fusion(f32[2048,224]{0,1:T(8,128)} %copy.71, f32[2048,224]{0,1:T(8,128)} %fusion.55, f32[224]{0:T(256)S(1)} %get-tuple-element.275), kind=kLoop, calls=%fused_computation.11.clone.1 | loop fusion | flops 2750464 | bytes 3679104 | tf_op jit(solution)/shard_map/while/body/eval_jaxpr/reduce_sum | solution.py:50
  174.5 2.7 %fusion.55 = f32[2048,224]{0,1:T(8,128)} fusion(bf16[64,224]{1,0:T(8,128)(2,1)S(1)} %get-tuple-element.273, f32[224]{0:T(256)S(1)} %get-tuple-element.274, bf16[2048,64]{0,1:T(8,128)(2,1)S(1)} %multiply_convert_fusion.3, bf16[64,64]{1,0:T(8,128)(2,1)S(1)} %get-tuple-element.271, f32[64]{0:T(128)S(1)} %get-tuple-element.272), kind=kOutput, calls=%fused_computation.10.clone.1 | convolution fusion | flops 79953920 | bytes 2135168 | tf_op jit(solution)/shard_map/while/body/eval_jaxpr/dot_general | solution.py:45
  183.4 2.8 %multiply_reduce_fusion.2 = f32[2048]{0:T(1024)S(1)} fusion(f32[2048,224]{0,1:T(8,128)} %copy.71, f32[2048,224]{0,1:T(8,128)} %fusion.55, f32[224]{0:T(256)S(1)} %get-tuple-element.275), kind=kLoop, calls=%fused_computation.11.clone.1 | loop fusion | flops 2750464 | bytes 3679104 | tf_op jit(solution)/shard_map/while/body/eval_jaxpr/reduce_sum | solution.py:50
  187.4 2.7 %fusion.55 = f32[2048,224]{0,1:T(8,128)} fusion(bf16[64,224]{1,0:T(8,128)(2,1)S(1)} %get-tuple-element.273, f32[224]{0:T(256)S(1)} %get-tuple-element.274, bf16[2048,64]{0,1:T(8,128)(2,1)S(1)} %multiply_convert_fusion.3, bf16[64,64]{1,0:T(8,128)(2,1)S(1)} %get-tuple-element.271, f32[64]{0:T(128)S(1)} %get-tuple-element.272), kind=kOutput, calls=%fused_computation.10.clone.1 | convolution fusion | flops 79953920 | bytes 2135168 | tf_op jit(solution)/shard_map/while/body/eval_jaxpr/dot_general | solution.py:45
  196.4 2.8 %multiply_reduce_fusion.2 = f32[2048]{0:T(1024)S(1)} fusion(f32[2048,224]{0,1:T(8,128)} %copy.71, f32[2048,224]{0,1:T(8,128)} %fusion.55, f32[224]{0:T(256)S(1)} %get-tuple-element.275), kind=kLoop, calls=%fused_computation.11.clone.1 | loop fusion | flops 2750464 | bytes 3679104 | tf_op jit(solution)/shard_map/while/body/eval_jaxpr/reduce_sum | solution.py:50
  201.1 1.9 collective-permute-start.9
  203.2 9.1 %collective-permute-done.9 = f32[16,768]{0,1:T(8,128)S(1)} collective-permute-done((f32[16,768]{0,1:T(8,128)S(1)}, f32[16,768]{0,1:T(8,128)S(1)}, u32[]{:S(2)}, u32[]{:S(2)}) %collective-permute-start.9) | collective-permute-done | bytes 49184 | tf_op jit(solution)/shard_map/ppermute | solution.py:31
  212.3 8.8 %scatter_custom_fusion = f32[16,2048]{0,1:T(8,128)S(1)} fusion(f32[16,2048]{0,1:T(8,128)S(1)} %bitcast.94, s32[1536]{0:T(1024)S(1)} %fusion.23, f32[768,16]{1,0:T(8,128)S(1)} %bitcast.96, f32[]{:T(128)} %constant.918, f32[768,16]{1,0:T(8,128)S(1)} %broadcast_select_fusion), kind=kCustom, calls=%fused_computation.44 | custom fusion | flops 49152 | bytes 917508 | tf_op jit(solution)/shard_map/scatter-add | solution.py:162
  (176 shorter events, 75.5 us)
Async XLA Ops:
  0.6 12.1 %copy-start = (f32[7,16,16,128]{3,2,1,0:T(8,128)S(1)}, f32[7,16,16,128]{3,2,1,0:T(8,128)}, u32[]{:S(2)}) copy-start(f32[7,16,16,128]{3,2,1,0:T(8,128)} %param.21) | copy-start | bytes 2752516
  0.6 19.6 %copy-start.10 = (s32[16]{0:T(128)S(1)}, s32[16]{0:T(128)}, u32[]{:S(2)}) copy-start(s32[16]{0:T(128)} %param.22) | copy-start | bytes 196
  0.7 22.7 %copy-start.9 = (s32[16]{0:T(128)S(1)}, s32[16]{0:T(128)}, u32[]{:S(2)}) copy-start(s32[16]{0:T(128)} %param.23) | copy-start | bytes 196
  0.7 35.9 %copy-start.8 = (s32[1,1,1536]{2,1,0:T(1,128)S(1)}, s32[1,1,1536]{2,1,0:T(1,128)}, u32[]{:S(2)}) copy-start(s32[1,1,1536]{2,1,0:T(1,128)} %param.34) | copy-start | bytes 18436
  0.7 36.0 %copy-start.12 = (s32[1,64]{1,0:T(1,128)S(1)}, s32[1,64]{1,0:T(1,128)}, u32[]{:S(2)}) copy-start(s32[1,64]{1,0:T(1,128)} %param.35) | copy-start | bytes 772
  0.7 39.0 %copy-start.18 = (f32[16]{0:T(128)S(1)}, f32[16]{0:T(128)}, u32[]{:S(2)}) copy-start(f32[16]{0:T(128)} %param.24) | copy-start | bytes 196
  0.7 39.6 %copy-start.13 = (f32[16]{0:T(128)S(1)}, f32[16]{0:T(128)}, u32[]{:S(2)}) copy-start(f32[16]{0:T(128)} %param.25) | copy-start | bytes 196
  3.8 36.7 %collective-permute-start = (f32[7,16,16,32]{3,2,1,0:T(8,128)}, f32[7,16,16,32]{3,2,1,0:T(8,128)S(1)}, u32[]{:S(2)}, u32[]{:S(2)}) collective-permute-start(f32[7,16,16,32]{3,2,1,0:T(8,128)} %get-tuple-element.163), channel_id=1, source_target_pairs={{12,0},{24,12},{36,24},{48,36},{60,48},{72,60},{84,72},{96,84},{10... | collective-permute-start | bytes 688136 | tf_op jit(solution)/shard_map/ppermute | solution.py:21
  10.8 29.7 %collective-permute-start.1 = (f32[7,16,16,32]{3,2,1,0:T(8,128)}, f32[7,16,16,32]{3,2,1,0:T(8,128)S(1)}, u32[]{:S(2)}, u32[]{:S(2)}) collective-permute-start(f32[7,16,16,32]{3,2,1,0:T(8,128)} %get-tuple-element.164), channel_id=1, source_target_pairs={{0,12},{12,24},{24,36},{36,48},{48,60},{60,72},{72,84},{84,96},{96... | collective-permute-start | bytes 688136 | tf_op jit(solution)/shard_map/ppermute | solution.py:19
  12.8 33.7 %collective-permute-start.2 = (f32[7,16,1,128]{3,2,1,0:T(1,128)S(1)}, f32[7,16,1,128]{3,2,1,0:T(1,128)S(1)}, u32[]{:S(2)}, u32[]{:S(2)}) collective-permute-start(f32[7,16,1,128]{3,2,1,0:T(1,128)S(1)} %get-tuple-element.165), channel_id=1, source_target_pairs={{1,0},{2,1},{3,2},{4,3},{5,4},{6,5},{7,6},{8,7},{9,8},{10,9},{11,1... | collective-permute-start | bytes 172040 | tf_op jit(solution)/shard_map/ppermute | solution.py:21
  14.7 31.8 %collective-permute-start.3 = (f32[7,16,1,128]{3,2,1,0:T(1,128)S(1)}, f32[7,16,1,128]{3,2,1,0:T(1,128)S(1)}, u32[]{:S(2)}, u32[]{:S(2)}) collective-permute-start(f32[7,16,1,128]{3,2,1,0:T(1,128)S(1)} %get-tuple-element.166), channel_id=1, source_target_pairs={{0,1},{1,2},{2,3},{3,4},{4,5},{5,6},{6,7},{7,8},{8,9},{9,10},{10,1... | collective-permute-start | bytes 172040 | tf_op jit(solution)/shard_map/ppermute | solution.py:19
  42.4 4.1 %copy-start.6 = (f32[7,16,16,128]{3,2,1,0:T(8,128)S(1)}, f32[7,16,16,128]{3,2,1,0:T(8,128)}, u32[]{:S(2)}) copy-start(f32[7,16,16,128]{3,2,1,0:T(8,128)} %param.20) | copy-start | bytes 2752516
  42.4 4.1 %copy-start.11 = (f32[16]{0:T(128)S(1)}, f32[16]{0:T(128)}, u32[]{:S(2)}) copy-start(f32[16]{0:T(128)} %param.26) | copy-start | bytes 196
  47.7 17.6 %collective-permute-start.4 = (f32[7,16,16,32]{3,2,1,0:T(8,128)S(1)}, f32[7,16,16,32]{3,2,1,0:T(8,128)S(1)}, u32[]{:S(2)}, u32[]{:S(2)}) collective-permute-start(f32[7,16,16,32]{3,2,1,0:T(8,128)S(1)} %get-tuple-element.157), channel_id=1, source_target_pairs={{12,0},{24,12},{36,24},{48,36},{60,48},{72,60},{84,72},{96,84},{10... | collective-permute-start | bytes 688136 | tf_op jit(solution)/shard_map/ppermute | solution.py:21
  54.4 18.0 %collective-permute-start.5 = (f32[7,16,16,32]{3,2,1,0:T(8,128)S(1)}, f32[7,16,16,32]{3,2,1,0:T(8,128)S(1)}, u32[]{:S(2)}, u32[]{:S(2)}) collective-permute-start(f32[7,16,16,32]{3,2,1,0:T(8,128)S(1)} %get-tuple-element.158), channel_id=1, source_target_pairs={{0,12},{12,24},{24,36},{36,48},{48,60},{60,72},{72,84},{84,96},{96... | collective-permute-start | bytes 688136 | tf_op jit(solution)/shard_map/ppermute | solution.py:19
  56.3 22.2 %collective-permute-start.6 = (f32[7,16,1,128]{3,2,1,0:T(1,128)S(1)}, f32[7,16,1,128]{3,2,1,0:T(1,128)S(1)}, u32[]{:S(2)}, u32[]{:S(2)}) collective-permute-start(f32[7,16,1,128]{3,2,1,0:T(1,128)S(1)} %get-tuple-element.153), channel_id=1, source_target_pairs={{1,0},{2,1},{3,2},{4,3},{5,4},{6,5},{7,6},{8,7},{9,8},{10,9},{11,1... | collective-permute-start | bytes 172040 | tf_op jit(solution)/shard_map/ppermute | solution.py:21
  58.2 20.3 %collective-permute-start.7 = (f32[7,16,1,128]{3,2,1,0:T(1,128)S(1)}, f32[7,16,1,128]{3,2,1,0:T(1,128)S(1)}, u32[]{:S(2)}, u32[]{:S(2)}) collective-permute-start(f32[7,16,1,128]{3,2,1,0:T(1,128)S(1)} %get-tuple-element.154), channel_id=1, source_target_pairs={{0,1},{1,2},{2,3},{3,4},{4,5},{5,6},{6,7},{7,8},{8,9},{9,10},{10,1... | collective-permute-start | bytes 172040 | tf_op jit(solution)/shard_map/ppermute | solution.py:19
  80.4 10.0 %copy-start.4 = (f32[7,16,16,128]{3,2,1,0:T(8,128)}, f32[7,16,16,128]{3,2,1,0:T(8,128)S(1)}, u32[]{:S(2)}) copy-start(f32[7,16,16,128]{3,2,1,0:T(8,128)S(1)} %get-tuple-element.118) | copy-start | bytes 2752516
  98.4 1.6 copy-start.1
  101.1 8.8 %collective-permute-start.8 = (bf16[7,16,768]{2,1,0:T(8,128)(2,1)S(1)}, bf16[7,16,768]{2,1,0:T(8,128)(2,1)S(1)}, u32[]{:S(2)}, u32[]{:S(2)}) collective-permute-start(bf16[7,16,768]{2,1,0:T(8,128)(2,1)S(1)} %copy.55), channel_id=1, source_target_pairs={{384,0},{396,12},{408,24},{420,36},{432,48},{444,60},{456,72},{468... | collective-permute-start | bytes 516104 | tf_op jit(solution)/shard_map/ppermute | solution.py:31
  131.5 2.9 %copy-start.3 = (bf16[6,7,16,128]{2,3,1,0:T(8,128)(2,1)S(1)}, bf16[6,7,16,128]{2,3,1,0:T(8,128)(2,1)}, u32[]{:S(2)}) copy-start(bf16[6,7,16,128]{2,3,1,0:T(8,128)(2,1)} %copy-done.2) | copy-start | bytes 516100 | tf_op jit(solution)/shard_map/while
  134.4 1.1 copy-start.2
  144.5 2.9 %copy-start.3 = (bf16[6,7,16,128]{2,3,1,0:T(8,128)(2,1)S(1)}, bf16[6,7,16,128]{2,3,1,0:T(8,128)(2,1)}, u32[]{:S(2)}) copy-start(bf16[6,7,16,128]{2,3,1,0:T(8,128)(2,1)} %copy-done.2) | copy-start | bytes 516100 | tf_op jit(solution)/shard_map/while
  147.4 1.1 copy-start.2
  157.5 2.9 %copy-start.3 = (bf16[6,7,16,128]{2,3,1,0:T(8,128)(2,1)S(1)}, bf16[6,7,16,128]{2,3,1,0:T(8,128)(2,1)}, u32[]{:S(2)}) copy-start(bf16[6,7,16,128]{2,3,1,0:T(8,128)(2,1)} %copy-done.2) | copy-start | bytes 516100 | tf_op jit(solution)/shard_map/while
  160.4 1.1 copy-start.2
  170.4 2.9 %copy-start.3 = (bf16[6,7,16,128]{2,3,1,0:T(8,128)(2,1)S(1)}, bf16[6,7,16,128]{2,3,1,0:T(8,128)(2,1)}, u32[]{:S(2)}) copy-start(bf16[6,7,16,128]{2,3,1,0:T(8,128)(2,1)} %copy-done.2) | copy-start | bytes 516100 | tf_op jit(solution)/shard_map/while
  173.4 1.1 copy-start.2
  183.4 2.9 %copy-start.3 = (bf16[6,7,16,128]{2,3,1,0:T(8,128)(2,1)S(1)}, bf16[6,7,16,128]{2,3,1,0:T(8,128)(2,1)}, u32[]{:S(2)}) copy-start(bf16[6,7,16,128]{2,3,1,0:T(8,128)(2,1)} %copy-done.2) | copy-start | bytes 516100 | tf_op jit(solution)/shard_map/while
  196.4 2.9 %copy-start.3 = (bf16[6,7,16,128]{2,3,1,0:T(8,128)(2,1)S(1)}, bf16[6,7,16,128]{2,3,1,0:T(8,128)(2,1)}, u32[]{:S(2)}) copy-start(bf16[6,7,16,128]{2,3,1,0:T(8,128)(2,1)} %copy-done.2) | copy-start | bytes 516100 | tf_op jit(solution)/shard_map/while
  199.3 12.9 %copy-start.5 = (f32[1,16,16,128]{1,3,2,0:T(8,128)S(1)}, f32[1,16,16,128]{1,3,2,0:T(8,128)}, u32[]{:S(2)}) copy-start(f32[1,16,16,128]{1,3,2,0:T(8,128)} %copy.53) | copy-start | bytes 393220
  201.1 11.2 %collective-permute-start.9 = (f32[16,768]{0,1:T(8,128)S(1)}, f32[16,768]{0,1:T(8,128)S(1)}, u32[]{:S(2)}, u32[]{:S(2)}) collective-permute-start(f32[16,768]{0,1:T(8,128)S(1)} %select_bitcast_fusion), channel_id=1, source_target_pairs={{384,0},{396,12},{408,24},{420,36},{432,48},{444,60},{456,72},{468... | collective-permute-start | bytes 147464 | tf_op jit(solution)/shard_map/ppermute | solution.py:31
  (9 other events, 7.3 us)
where the time goes:
time: 223 us; the launch traced here: 222 us
  local copies, waits for them, and re-layouts  68.6 us (31%)
  other arithmetic  58.9 us (26%)
  starting transfers between devices  36.2 us (16%)
  waiting for transfers between devices  22.2 us (10%)
  matrix products  18.5 us (8%)
  between operations  17.1 us (8%)
    another operation x12, local copies, waits for them, and re-layouts, absorb(): depth = jnp.cumsum(tau, axis=1)  18.4 us
    ppermute x4, starting transfers between devices, extended(): lax.ppermute(head, axis, [((i + 1) % count, i) for i in range(ends)])  17.5 us
    reduce_sum x6, other arithmetic, absorb(): return jnp.sum((jnp.exp(-above) - jnp.exp(-depth)) * band_weight, axis=-1)  16.8 us
    dot_general x6, matrix products, absorb(): jnp.dot(second, w_third, preferred_element_type=jnp.float32) + b_third  16.4 us
    ppermute x4, starting transfers between devices, extended(): lax.ppermute(tail, axis, [(i, (i + 1) % count) for i in range(ends)])  14.6 us
    ppermute x2, waiting for transfers between devices, shifted_2(): return lax.ppermute(block, axis, route)  13.4 us
    mul x6, local copies, waits for them, and re-layouts, absorb(): 0.15 * jax.nn.softplus(jnp.dot(second, w_third, preferred_element_type=jn...  11.2 us
    scatter-add x1, other arithmetic, body(): temper = now[2].reshape(now.shape[1], cells).at[:, listed].add(heat.T)  8.76 us
  transfers between devices with their start and end apart: 10, of which 4 were waited for; matrix products, arithmetic and copies ran while one was open for 9% of the time, Pallas kernels for 0%

commit v1 on v0

v1 whole, which is shorter than its diff:
```python
import functools

import jax
import jax.numpy as jnp
from jax import lax
from jax.experimental import pallas as pl
from jax.experimental.pallas import tpu as pltpu
from jax.sharding import PartitionSpec as P

VARS = 7
LEV = 16
ROWS = 16
LANES = 128
POLAR = 4
HID = 64
GPT = 224
LISTED = 1536
TILES_POLAR = VARS * LEV // 2
TILES_COLS = 16
LON_ROWS = 8 * (TILES_POLAR + TILES_COLS)
LAT_NOW = VARS * 4
LAT_PREV = VARS * 2
LAT_ROWS = 8 * (LAT_NOW + LAT_PREV + 1)
LOG2E = 1.4426950408889634
TAU_SCALE = 0.15

f32 = jnp.float32
bf16 = jnp.bfloat16


def iotas():
    lane = lax.broadcasted_iota(jnp.int32, (8, LANES), 1)
    sub = lax.broadcasted_iota(jnp.int32, (8, LANES), 0)
    return lane, sub


def roll_lanes(x, shift):
    return pltpu.roll(x, shift, 1)


def roll_subs(x, shift):
    return pltpu.roll(x, shift, 0)


def pick(x, index):
    return jnp.take_along_axis(x, index, axis=1, mode="promise_in_bounds")


def col_tile(which, half, group):
    return 8 * (TILES_POLAR + which * 8 + half * 4 + group)


def pack_kernel(first_ref, now_ref, prev_ref, zc_ref, east_ref, west_ref, north_ref, south_ref):
    lane, sub = iotas()
    first = first_ref[0]
    base = pl.multiple_of(jnp.where(first == 1, 0, 8), 8)
    turn = jnp.where(first == 1, 0, 4)
    extra = jnp.where(first == 1, 4, 11)

    def polar(k, carry):
        for v in range(VARS):
            east = []
            west = []
            for part in range(2):
                level = k + 8 * part
                amount = (4 * part + turn) % 8
                tile = roll_subs(now_ref[v, level, pl.ds(base, 8), :], amount)
                old = roll_lanes(roll_subs(prev_ref[v, level, pl.ds(base, 8), :], amount), 64)
                row = jnp.broadcast_to(now_ref[v, level, pl.ds(extra, 1), :], (8, LANES))
                east.append(
                    jnp.where(lane >= 64, tile, jnp.where(lane >= 32, old, roll_lanes(row, 32)))
                )
                west.append(
                    jnp.where(lane < 64, tile, jnp.where(lane < 96, old, roll_lanes(row, 96)))
                )
            at = pl.multiple_of((v * 8 + k) * 8, 8)
            east_ref[pl.ds(at, 8), :] = jnp.where(sub < 4, east[0], east[1])
            west_ref[pl.ds(at, 8), :] = jnp.where(sub < 4, west[0], west[1])
        return carry

    lax.fori_loop(0, 8, polar, 0)

    for group in range(4):
        members = [v for v in (2 * group, 2 * group + 1) if v < VARS]

        def columns(k, tiles):
            tiles = list(tiles)
            for v in members:
                at = (v % 2) * 64 + 4 * k
                low = (lane == at) | (lane == at + 1)
                high = (lane == at + 2) | (lane == at + 3)
                for which, ref in enumerate((now_ref, prev_ref)):
                    for half in range(2):
                        x = ref[v, k, pl.ds(8 * half, 8), :]
                        slot = 4 * which + 2 * half
                        tiles[slot] = jnp.where(low, roll_lanes(x, at), tiles[slot])
                        tiles[slot + 1] = jnp.where(
                            high, roll_lanes(x, (at + 4) % LANES), tiles[slot + 1]
                        )
            return tuple(tiles)

        zero = jnp.zeros((8, LANES), f32)
        tiles = lax.fori_loop(0, LEV, columns, (zero,) * 8)
        for which in range(2):
            for half in range(2):
                at = col_tile(which, half, group)
                west_ref[at : at + 8, :] = tiles[4 * which + 2 * half]
                east_ref[at : at + 8, :] = tiles[4 * which + 2 * half + 1]

    def rows_now(g, carry):
        for v in range(VARS):
            north = None
            south = None
            for h in range(4):
                up = now_ref[v, g + 4 * h, 0:8, :]
                down = now_ref[v, g + 4 * h, 8:16, :]
                up = roll_subs(up, 2 * h) if h else up
                down = roll_subs(down, (2 * h + 2) % 8) if h != 3 else down
                mask = sub >= 2 * h
                north = up if h == 0 else jnp.where(mask, up, north)
                south = down if h == 0 else jnp.where(mask, down, south)
            at = pl.multiple_of((v * 4 + g) * 8, 8)
            north_ref[pl.ds(at, 8), :] = north
            south_ref[pl.ds(at, 8), :] = south
        return carry

    lax.fori_loop(0, 4, rows_now, 0)

    def rows_prev(g, carry):
        for v in range(VARS):
            north = None
            south = None
            for h in range(8):
                up = prev_ref[v, g + 2 * h, 0:8, :]
                down = prev_ref[v, g + 2 * h, 8:16, :]
                up = roll_subs(up, h) if h else up
                down = roll_subs(down, h + 1) if h != 7 else down
                mask = sub >= h
                north = up if h == 0 else jnp.where(mask, up, north)
                south = down if h == 0 else jnp.where(mask, down, south)
            at = pl.multiple_of((LAT_NOW + v * 2 + g) * 8, 8)
            north_ref[pl.ds(at, 8), :] = north
            south_ref[pl.ds(at, 8), :] = south
        return carry

    lax.fori_loop(0, 2, rows_prev, 0)
    north_ref[LAT_ROWS - 8 :, :] = jnp.broadcast_to(zc_ref[0:1, :], (8, LANES))
    south_ref[LAT_ROWS - 8 :, :] = jnp.broadcast_to(zc_ref[15:16, :], (8, LANES))


def main_kernel(
    first_ref,
    count_ref,
    merid_ref,
    filter_ref,
    now_ref,
    prev_ref,
    fromwest_ref,
    fromeast_ref,
    fromnorth_ref,
    fromsouth_ref,
    stride_ref,
    flen_ref,
    zc_ref,
    listed_ref,
    w1_ref,
    b1_ref,
    w2_ref,
    b2_ref,
    w3_ref,
    b3_ref,
    start_ref,
    prev_out,
    now_out,
    outp_ref,
    outn_ref,
    feats_ref,
    pstar_ref,
    h1_ref,
    h2_ref,
    part_ref,
    mask_ref,
    sems,
    last_sem,
):
    lane, sub = iotas()
    first = first_ref[0]
    polar_base = jnp.where(first == 1, 0, 4)
    east_cols = (lane % 4) < 2
    for i in range(TILES_COLS):
        at = 8 * (TILES_POLAR + i)
        pstar_ref[8 * i : 8 * i + 8, :] = jnp.where(
            east_cols, fromeast_ref[at : at + 8, :], fromwest_ref[at : at + 8, :]
        )
    corner = []
    for group in range(4):
        at = LAT_ROWS - 8 + group
        corner.append(
            jnp.where(
                sub == 7,
                jnp.broadcast_to(fromnorth_ref[at : at + 1, :], (8, LANES)),
                jnp.broadcast_to(fromsouth_ref[at : at + 1, :], (8, LANES)),
            )
        )
    at = LAT_ROWS - 4
    zc_outer = jnp.where(
        sub == 7,
        jnp.broadcast_to(fromnorth_ref[at : at + 1, :], (8, LANES)),
        jnp.broadcast_to(fromsouth_ref[at : at + 1, :], (8, LANES)),
    )
    col_offset = jnp.where(
        lane < 64, jnp.minimum(lane, 1), jnp.maximum(lane, 126) - 124
    )
    edge = (lane < 2) | (lane >= 126)
    usecol = [edge | (first != 1), edge | (first == 1)]
    is_polar = (sub >= polar_base) & (sub < polar_base + 4)
    swap = jnp.where(lane < 64, lane + 96, lane - 96) % LANES

    def shifts(amount):
        return (
            (lane + amount) % LANES,
            lane < amount,
            (lane - amount) % LANES,
            lane >= LANES - amount,
        )

    s_tab = [shifts(stride_ref[0:8, :]), shifts(stride_ref[8:16, :])]
    m_tab = [shifts(flen_ref[0:8, :]), shifts(flen_ref[8:16, :])]
    one_tab = shifts(jnp.ones((8, LANES), jnp.int32))
    cz = [
        zc_ref[0:8, :] * (1.0 / stride_ref[0:8, :].astype(f32)),
        zc_ref[8:16, :] * (1.0 / stride_ref[8:16, :].astype(f32)),
    ]

    def ahead(x, other, tab):
        return pick(jnp.where(tab[1], other, x), tab[0])

    def behind(x, other, tab):
        return pick(jnp.where(tab[3], other, x), tab[2])

    def merid_of(t0, t1, t2, last):
        u0, u1, u2 = (roll_subs(t, 7) for t in (t0, t1, t2))
        d0, d1, d2 = (roll_subs(t, 1) for t in (t0, t1, t2))
        bottom = sub == 7
        top = sub == 0
        out = [
            jnp.where(bottom, u1, u0) - jnp.where(top, d2, d0),
            jnp.where(bottom, u2, u1) - jnp.where(top, d0, d1),
        ]
        if last:
            out.append(jnp.where(bottom, u0, u2) - jnp.where(top, d1, d2))
        return out

    def level(k, carry):
        mc = merid_ref[k]
        fc = filter_ref[k]
        pol_at = 8 * (k % 8)
        pol_turn = (polar_base + 8 - 4 * (k // 8)) % 8
        gn, hn = k % 4, k // 4
        gp, hp = k % 2, k // 2

        def gather_tiles(v):
            group = v // 2
            index = col_offset + (v % 2) * 64 + 4 * k
            cells = [now_ref[v, k, 0:8, :], now_ref[v, k, 8:16, :]]
            old = [prev_ref[v, k, 0:8, :], prev_ref[v, k, 8:16, :]]
            at = pl.multiple_of((v * 4 + gn) * 8, 8)
            t2 = jnp.where(
                sub >= 4,
                roll_subs(fromnorth_ref[pl.ds(at, 8), :], (14 - 2 * hn) % 8),
                roll_subs(fromsouth_ref[pl.ds(at, 8), :], (8 - 2 * hn) % 8),
            )
            at = pl.multiple_of((LAT_NOW + v * 2 + gp) * 8, 8)
            t2_old = jnp.where(
                sub >= 4,
                roll_subs(fromnorth_ref[pl.ds(at, 8), :], 7 - hp),
                roll_subs(fromsouth_ref[pl.ds(at, 8), :], (8 - hp) % 8),
            )
            at = pl.multiple_of(v * 64 + pol_at, 8)
            te = fromeast_ref[pl.ds(at, 8), :]
            tw = fromwest_ref[pl.ds(at, 8), :]
            natural = roll_subs(jnp.where(lane < 64, te, tw), pol_turn)
            crossed = roll_subs(jnp.where(lane < 64, tw, te), pol_turn)
            strip = jnp.where(is_polar, natural, roll_subs(pick(crossed, swap), 4))
            strip_old = roll_lanes(crossed, 64)
            halo = []
            halo_old = []
            for half in range(2):
                tile = 8 * (half * 4 + group)
                halo.append(
                    jnp.where(usecol[half], pick(pstar_ref[tile : tile + 8, :], index), strip)
                )
                tile = tile + 64
                halo_old.append(
                    jnp.where(usecol[half], pick(pstar_ref[tile : tile + 8, :], index), strip_old)
                )
            t2_halo = pick(corner[group], index)
            return cells, old, t2, t2_old, halo, halo_old, t2_halo

        tiles = [gather_tiles(v) for v in range(VARS)]
        u, w = tiles[0], tiles[1]
        cu_c = [cz[h] * u[0][h] for h in range(2)] + [zc_outer * u[2]]
        cv_c = [mc * w[0][h] for h in range(2)] + [mc * w[2]]
        cu_h = [cz[h] * u[4][h] for h in range(2)]
        cv_h = [mc * w[4][h] for h in range(2)]

        def tend(x, other, merid, cu, cv, s, m):
            zonal = ahead(x, other, s) - behind(x, other, s)
            second = ahead(x, other, m) + behind(x, other, m) - 2.0 * x
            return fc * second - cu * zonal - cv * merid

        fresh = []
        for v in range(VARS):
            cells, old, t2, t2_old, halo, halo_old, t2_halo = tiles[v]
            md = merid_of(cells[0], cells[1], t2, True)
            mh = merid_of(halo[0], halo[1], t2_halo, False)
            new = []
            new_halo = []
            filtered = []
            for h in range(2):
                x, o = cells[h], halo[h]
                n = old[h] + tend(x, o, md[h], cu_c[h], cv_c[h], s_tab[h], m_tab[h])
                new.append(n)
                filtered.append(x + 0.1 * (old[h] - 2.0 * x + n))
                new_halo.append(
                    halo_old[h] + tend(o, x, mh[h], cu_h[h], cv_h[h], s_tab[h], m_tab[h])
                )
            right = ahead(t2, t2_halo, one_tab)
            left = behind(t2, t2_halo, one_tab)
            new_t2 = t2_old + (
                fc * (right + left - 2.0 * t2) - cu_c[2] * (right - left) - cv_c[2] * md[2]
            )
            fresh.append((new, new_halo, new_t2, filtered))

        cu = [cz[h] * fresh[0][0][h] for h in range(2)]
        cv = [mc * fresh[1][0][h] for h in range(2)]
        for v in range(VARS):
            new, new_halo, new_t2, filtered = fresh[v]
            md = merid_of(new[0], new[1], new_t2, False)
            both = []
            for h in range(2):
                x = new[h]
                n = filtered[h] + tend(x, new_halo[h], md[h], cu[h], cv[h], s_tab[h], m_tab[h])
                outn_ref[v, k, 8 * h : 8 * h + 8, :] = n
                outp_ref[v, k, 8 * h : 8 * h + 8, :] = x + 0.1 * (filtered[h] - 2.0 * x + n)
                both.append(n)
            feats_ref[k, 16 * v : 16 * v + 16, :] = jnp.concatenate(both, axis=0).astype(bf16)
        pltpu.make_async_copy(outp_ref.at[:, k], prev_out.at[:, k], sems.at[k, 0]).start()
        pltpu.make_async_copy(outn_ref.at[0:2, k], now_out.at[0:2, k], sems.at[k, 1]).start()
        pltpu.make_async_copy(outn_ref.at[3:7, k], now_out.at[3:7, k], sems.at[k, 2]).start()
        return carry

    lax.fori_loop(0, LEV, level, 0)

    listed = listed_ref[...]
    live = lax.broadcasted_iota(jnp.int32, (1, LISTED), 1) < count_ref[0]
    row_hot = (listed // LANES == lax.broadcasted_iota(jnp.int32, (ROWS, LISTED), 0)) & live
    col_hot = listed % LANES == lax.broadcasted_iota(jnp.int32, (LANES, LISTED), 0)
    mask_ref[...] = lax.dot_general(
        jnp.where(row_hot, 1.0, 0.0).astype(bf16),
        jnp.where(col_hot, 1.0, 0.0).astype(bf16),
        (((1,), (1,)), ((), ())),
        preferred_element_type=f32,
    )

    column = lax.broadcasted_iota(jnp.int32, (HID, VARS * ROWS), 1) % ROWS
    start_sum = None
    for i in range(GPT // 8):
        t = jnp.exp2(-TAU_SCALE * start_ref[8 * i : 8 * i + 8, :])
        start_sum = t if start_sum is None else start_sum + t
    half_g = GPT // 2

    def network(r, carry):
        w1 = jnp.where(column == r, w1_ref[...], 0.0).astype(bf16)
        for k in range(LEV):
            z = jnp.dot(w1, feats_ref[k], preferred_element_type=f32) + b1_ref[...]
            h1_ref[k] = (z * jnp.tanh(z) + z).astype(bf16)
        for k in range(LEV):
            z = jnp.dot(w2_ref[...], h1_ref[k], preferred_element_type=f32) + b2_ref[...]
            h2_ref[k] = (z * jnp.tanh(z) + z).astype(bf16)
        for part in range(2):
            at = part * half_g
            total = start_ref[at : at + half_g, :]
            for k in range(LEV):
                y = jnp.dot(w3_ref[at : at + half_g, :], h2_ref[k], preferred_element_type=f32)
                y = y * LOG2E + b3_ref[at : at + half_g, :]
                e = jnp.exp2(jnp.minimum(y, 126.0))
                total = total + jnp.maximum(y, jnp.log2(1.0 + e))
                t = jnp.exp2(-TAU_SCALE * total)
                s = t[0:8]
                for i in range(1, half_g // 8):
                    s = s + t[8 * i : 8 * i + 8]
                if part == 0:
                    part_ref[k] = s
                else:
                    part_ref[k] = part_ref[k] + s
        lit = mask_ref[pl.ds(r, 1), :] > 0.5
        before = start_sum
        for k in range(LEV):
            after = part_ref[k]
            heat = jnp.sum(before - after, axis=0, keepdims=True)
            before = after
            outn_ref[2, k, pl.ds(r, 1), :] = outn_ref[2, k, pl.ds(r, 1), :] + jnp.where(
                lit, heat, 0.0
            )
        return carry

    lax.fori_loop(0, ROWS, network, 0)
    last = pltpu.make_async_copy(outn_ref.at[2], now_out.at[2], last_sem)
    last.start()

    def drain(k, carry):
        pltpu.make_async_copy(outp_ref.at[:, k], prev_out.at[:, k], sems.at[k, 0]).wait()
        pltpu.make_async_copy(outn_ref.at[0:2, k], now_out.at[0:2, k], sems.at[k, 1]).wait()
        pltpu.make_async_copy(outn_ref.at[3:7, k], now_out.at[3:7, k], sems.at[k, 2]).wait()
        return carry

    lax.fori_loop(0, LEV, drain, 0)
    last.wait()


VMEM = pl.BlockSpec(memory_space=pltpu.VMEM)
SMEM = pl.BlockSpec(memory_space=pltpu.SMEM)
ANY = pl.BlockSpec(memory_space=pl.ANY)


def body(
    state_prev,
    state_now,
    stride_table,
    filter_len,
    zonal_coef,
    merid_coef,
    filter_coef,
    w_first,
    b_first,
    w_second,
    b_second,
    w_third,
    b_third,
    band_weight,
    sunlit_cols,
    sunlit_count,
):
    first = (lax.axis_index("lat") == 0).astype(jnp.int32).reshape(1)
    zc = jnp.broadcast_to(zonal_coef[:, None], (ROWS, LANES))
    stride = jnp.broadcast_to(stride_table[:, None], (ROWS, LANES))
    flen = jnp.broadcast_to(filter_len[:, None], (ROWS, LANES))
    count = lax.dynamic_slice(sunlit_count.reshape(-1), (lax.axis_index("lon"),), (1,))

    lon_shape = jax.ShapeDtypeStruct((LON_ROWS, LANES), f32)
    lat_shape = jax.ShapeDtypeStruct((LAT_ROWS, LANES), f32)
    east, west, north, south = pl.pallas_call(
        pack_kernel,
        name="pack",
        out_shape=(lon_shape, lon_shape, lat_shape, lat_shape),
        in_specs=[SMEM, VMEM, VMEM, VMEM],
        out_specs=(VMEM,) * 4,
        compiler_params=pltpu.CompilerParams(vmem_limit_bytes=16 << 20),
    )(first, state_now, state_prev, zc)

    nlon = lax.axis_size("lon")
    nlat = lax.axis_size("lat")
    fromwest = lax.ppermute(east, "lon", [(i, (i + 1) % nlon) for i in range(nlon)])
    fromeast = lax.ppermute(west, "lon", [((i + 1) % nlon, i) for i in range(nlon)])

    east_cols = (jnp.arange(LANES) % 4 < 2)[None, :]

    def corners(half, row):
        at = col_tile(0, half, 0)
        pieces = [
            x[at : at + 32].reshape(4, 8, LANES)[:, row] for x in (fromeast, fromwest)
        ]
        return jnp.where(east_cols, pieces[0], pieces[1])

    north = lax.dynamic_update_slice(north, corners(0, 0), (LAT_ROWS - 8, 0))
    south = lax.dynamic_update_slice(south, corners(1, 7), (LAT_ROWS - 8, 0))
    fromnorth = lax.ppermute(south, "lat", [(i, i + 1) for i in range(nlat - 1)])
    fromsouth = lax.ppermute(north, "lat", [(i + 1, i) for i in range(nlat - 1)])

    def wide(vector):
        return jnp.broadcast_to(vector[:, None], (vector.shape[0], LANES))

    w1 = jnp.repeat(w_first.T.astype(f32) * 0.5, ROWS, axis=1)
    w2 = (w_second.T.astype(f32) * 0.5).astype(bf16)
    w3 = w_third.T
    b1 = wide(b_first * 0.5)
    b2 = wide(b_second * 0.5)
    b3 = wide(b_third * LOG2E)
    start = wide(jnp.log2(band_weight) * (-1.0 / TAU_SCALE))

    state = jax.ShapeDtypeStruct(state_now.shape, f32)
    prev_out, now_out = pl.pallas_call(
        main_kernel,
        name="main",
        out_shape=(state, state),
        in_specs=[SMEM] * 4 + [VMEM] * 17,
        out_specs=(ANY, ANY),
        scratch_shapes=[
            pltpu.VMEM(state_now.shape, f32),
            pltpu.VMEM(state_now.shape, f32),
            pltpu.VMEM((LEV, VARS * ROWS, LANES), bf16),
            pltpu.VMEM((8 * TILES_COLS, LANES), f32),
            pltpu.VMEM((LEV, HID, LANES), bf16),
            pltpu.VMEM((LEV, HID, LANES), bf16),
            pltpu.VMEM((LEV, 8, LANES), f32),
            pltpu.VMEM((ROWS, LANES), f32),
            pltpu.SemaphoreType.DMA((LEV, 3)),
            pltpu.SemaphoreType.DMA,
        ],
        compiler_params=pltpu.CompilerParams(vmem_limit_bytes=36 << 20),
    )(
        first,
        count,
        merid_coef,
        filter_coef,
        state_now,
        state_prev,
        fromwest,
        fromeast,
        fromnorth,
        fromsouth,
        stride,
        flen,
        zc,
        sunlit_cols.reshape(1, LISTED),
        w1,
        b1,
        w2,
        b2,
        w3,
        b3,
        start,
    )
    return prev_out, now_out


def solution(mesh):
    in_specs = (
        P(None, None, "lat", "lon"),
        P(None, None, "lat", "lon"),
        P("lat"),
        P("lat"),
        P("lat"),
        P(),
        P(),
        P(),
        P(),
        P(),
        P(),
        P(),
        P(),
        P(),
        P("lat", "lon", None),
        P("lat", None),
    )
    out_specs = (P(None, None, "lat", "lon"), P(None, None, "lat", "lon"))
    return jax.shard_map(body, mesh=mesh, in_specs=in_specs, out_specs=out_specs, check_vma=False)
```

time: 223 us -> 78.7 us (0.35)
  the two profiles are of different devices: /device:TPU:192 before, /device:TPU:64 now
where the time goes in v1:
time: 78.7 us; the launch traced here: 78.3 us
  Pallas kernels  41.1 us (52%)
  starting transfers between devices  21.3 us (27%)
  waiting for transfers between devices  7.84 us (10%)
  local copies, waits for them, and re-layouts  7.02 us (9%)
  between operations  0.92 us (1%)
    pallas_call x1, Pallas kernels, body(): pl.pallas_call(main_kernel, name='main', out_shape=(state, state), in_spe...  34.6 us
    ppermute x1, starting transfers between devices, body(): lax.ppermute(north, 'lat', [(i + 1, i) for i in range(nlat - 1)])  10.5 us
    ppermute x1, starting transfers between devices, body(): lax.ppermute(west, 'lon', [((i + 1) % nlon, i) for i in range(nlon)])  7.01 us
    pallas_call x1, Pallas kernels, body(): pl.pallas_call(pack_kernel, name='pack', out_shape=(lon_shape, lon_shape,...  6.47 us
    unnamed x38, local copies, waits for them, and re-layouts  5.8 us
    ppermute x1, waiting for transfers between devices, body(): lax.ppermute(south, 'lat', [(i, i + 1) for i in range(nlat - 1)])  4.4 us
    ppermute x1, starting transfers between devices, body(): lax.ppermute(east, 'lon', [(i, (i + 1) % nlon) for i in range(nlon)])  1.92 us
    ppermute x1, starting transfers between devices, body(): lax.ppermute(south, 'lat', [(i, i + 1) for i in range(nlat - 1)])  1.92 us
  transfers between devices with their start and end apart: 4, of which 4 were waited for; matrix products, arithmetic and copies ran while one was open for 1% of the time, Pallas kernels for 0%

profile of v1, /device:TPU:64, one launch (start us, length us, event | category | flops | bytes accessed | tf_op | source)
XLA Modules:
  0.0 78.3 jit_solution(1728735136681883434)
XLA Ops:
  0.6 0.0 copy-start
  0.7 0.6 copy-done.13
  1.3 0.1 broadcast_in_dim.29.zc_ref
  1.4 1.2 %copy-done.1 = f32[7,16,16,128]{3,2,1,0:T(8,128)S(1)} copy-done((f32[7,16,16,128]{3,2,1,0:T(8,128)S(1)}, f32[7,16,16,128]{3,2,1,0:T(8,128)}, u32[]{:S(2)}) %copy-start.1) | copy-done | bytes 917528
  2.6 1.2 %copy-done.3 = f32[7,16,16,128]{3,2,1,0:T(8,128)S(1)} copy-done((f32[7,16,16,128]{3,2,1,0:T(8,128)S(1)}, f32[7,16,16,128]{3,2,1,0:T(8,128)}, u32[]{:S(2)}) %copy-start.3) | copy-done | bytes 917528
  3.8 6.5 %pack.1 = (f32[576,128]{1,0:T(8,128)S(1)}, f32[576,128]{1,0:T(8,128)S(1)}, f32[344,128]{1,0:T(8,128)S(1)}, f32[344,128]{1,0:T(8,128)S(1)}) custom-call(s32[1]{0:T(128)} %bitcast.first_ref, f32[7,16,16,128]{3,2,1,0:T(8,128)S(1)} %copy-done.1, f32[7,16,16,128]{3,2,1,0:T(8,128)S(1)} %copy-done.3, f32[16,128]{1,0:T(8,128)S(1)} %broadcast_in_dim.29.zc_ref), custom_call_target="tpu_custom_call" | custom-call | tf_op jit(solution)/shard_map/pack/pallas_call | solution.py:453
  10.3 1.9 %collective-permute-start = (f32[576,128]{1,0:T(8,128)S(1)}, f32[576,128]{1,0:T(8,128)S(1)}, u32[]{:S(2)}, u32[]{:S(2)}) collective-permute-start(f32[576,128]{1,0:T(8,128)S(1)} %get-tuple-element.6), channel_id=1, source_target_pairs={{0,12},{12,24},{24,36},{36,48},{48,60},{60,72},{72,84},{84,96},{96... | collective-permute-start | bytes 884744 | tf_op jit(solution)/shard_map/ppermute | solution.py:464
  12.2 7.0 %collective-permute-start.1 = (f32[576,128]{1,0:T(8,128)S(1)}, f32[576,128]{1,0:T(8,128)S(1)}, u32[]{:S(2)}, u32[]{:S(2)}) collective-permute-start(f32[576,128]{1,0:T(8,128)S(1)} %get-tuple-element.7), channel_id=1, source_target_pairs={{12,0},{24,12},{36,24},{48,36},{60,48},{72,60},{84,72},{96,84},{10... | collective-permute-start | bytes 884744 | tf_op jit(solution)/shard_map/ppermute | solution.py:465
  19.3 0.1 copy.25
  19.4 0.0 copy-start.8
  19.4 0.1 copy.27.w1_ref
  19.5 0.7 copy-done.8
  20.2 0.1 copy.26
  20.3 0.6 constant_dynamic-slice_fusion
  20.9 0.1 copy-done.16
  21.0 0.7 collective-permute-done.fromwest_ref
  21.7 1.7 %collective-permute-done.1.fromeast_ref = f32[576,128]{1,0:T(8,128)S(1)} collective-permute-done((f32[576,128]{1,0:T(8,128)S(1)}, f32[576,128]{1,0:T(8,128)S(1)}, u32[]{:S(2)}, u32[]{:S(2)}) %collective-permute-start.1) | collective-permute-done | bytes 294944 | tf_op jit(solution)/shard_map/ppermute | solution.py:465
  23.5 0.0 copy-start.17
  23.5 10.5 %collective-permute-start.3 = (f32[344,128]{1,0:T(8,128)S(1)}, f32[344,128]{1,0:T(8,128)S(1)}, u32[]{:S(2)}, u32[]{:S(2)}) collective-permute-start(f32[344,128]{1,0:T(8,128)S(1)} %get-tuple-element.14), channel_id=1, source_target_pairs={{1,0},{2,1},{3,2},{4,3},{5,4},{6,5},{7,6},{8,7},{9,8},{10,9},{11,1... | collective-permute-start | bytes 528392 | tf_op jit(solution)/shard_map/ppermute | solution.py:479
  34.0 1.9 %collective-permute-start.2 = (f32[344,128]{1,0:T(8,128)S(1)}, f32[344,128]{1,0:T(8,128)S(1)}, u32[]{:S(2)}, u32[]{:S(2)}) collective-permute-start(f32[344,128]{1,0:T(8,128)S(1)} %get-tuple-element.15), channel_id=1, source_target_pairs={{0,1},{1,2},{2,3},{3,4},{4,5},{5,6},{6,7},{7,8},{8,9},{9,10},{10,1... | collective-permute-start | bytes 528392 | tf_op jit(solution)/shard_map/ppermute | solution.py:478
  35.9 1.0 %collective-permute-done.3.fromsouth_ref = f32[344,128]{1,0:T(8,128)S(1)} collective-permute-done((f32[344,128]{1,0:T(8,128)S(1)}, f32[344,128]{1,0:T(8,128)S(1)}, u32[]{:S(2)}, u32[]{:S(2)}) %collective-permute-start.3) | collective-permute-done | bytes 176160 | tf_op jit(solution)/shard_map/ppermute | solution.py:479
  36.9 4.4 %collective-permute-done.2.fromnorth_ref = f32[344,128]{1,0:T(8,128)S(1)} collective-permute-done((f32[344,128]{1,0:T(8,128)S(1)}, f32[344,128]{1,0:T(8,128)S(1)}, u32[]{:S(2)}, u32[]{:S(2)}) %collective-permute-start.2) | collective-permute-done | bytes 176160 | tf_op jit(solution)/shard_map/ppermute | solution.py:478
  41.3 0.7 copy-done.14
  42.0 0.1 broadcast_in_dim.31.stride_ref
  42.0 0.6 copy-done.15
  42.6 0.1 broadcast_in_dim.32.flen_ref
  42.7 0.1 broadcast_in_dim.35.b2_ref
  42.8 0.1 broadcast_in_dim.34.b1_ref
  42.8 0.1 broadcast_in_dim.67.start_ref
  43.0 0.1 broadcast_in_dim.66.b3_ref
  43.1 0.6 copy-done.5
  43.6 34.6 %main.1 = (f32[7,16,16,128]{3,2,1,0:T(8,128)}, f32[7,16,16,128]{3,2,1,0:T(8,128)}) custom-call(s32[1]{0:T(128)} %bitcast.first_ref, s32[1]{0:T(128)} %bitcast.1.count_ref, f32[16]{0:T(128)S(1)} %copy-done.6, f32[16]{0:T(128)S(1)} %copy-done.7, f32[7,16,16,128]{3,2,1,0:T(8,128)S(1)} %copy-done.2, f32[7,16,16,128]{3,2,1,0:T(8,128)S(1)} %copy-done.4, ...), custom_call_target="tpu_custom_call" | custom-call | tf_op jit(solution)/shard_map/main/pallas_call | solution.py:493
  (40 shorter events, 0.1 us)
Async XLA Ops:
  0.6 19.7 %copy-start = (s32[1,64]{1,0:T(1,128)S(1)}, s32[1,64]{1,0:T(1,128)}, u32[]{:S(2)}) copy-start(s32[1,64]{1,0:T(1,128)} %param.31) | copy-start | bytes 772
  0.7 0.7 copy-start.13
  1.4 1.2 %copy-start.1 = (f32[7,16,16,128]{3,2,1,0:T(8,128)S(1)}, f32[7,16,16,128]{3,2,1,0:T(8,128)}, u32[]{:S(2)}) copy-start(f32[7,16,16,128]{3,2,1,0:T(8,128)} %now_ref.3) | copy-start | bytes 2752516
  2.6 1.2 %copy-start.3 = (f32[7,16,16,128]{3,2,1,0:T(8,128)S(1)}, f32[7,16,16,128]{3,2,1,0:T(8,128)}, u32[]{:S(2)}) copy-start(f32[7,16,16,128]{3,2,1,0:T(8,128)} %prev_ref.3) | copy-start | bytes 2752516
  3.7 15.5 %copy-start.11 = (f32[224]{0:T(256)S(1)}, f32[224]{0:T(256)}, u32[]{:S(2)}) copy-start(f32[224]{0:T(256)} %param.28) | copy-start | bytes 2692
  3.7 15.5 %copy-start.12 = (f32[224]{0:T(256)S(1)}, f32[224]{0:T(256)}, u32[]{:S(2)}) copy-start(f32[224]{0:T(256)} %param.29) | copy-start | bytes 2692
  3.7 15.5 %copy-start.10 = (bf16[7,64]{1,0:T(8,128)(2,1)S(1)}, bf16[7,64]{1,0:T(8,128)(2,1)}, u32[]{:S(2)}) copy-start(bf16[7,64]{1,0:T(8,128)(2,1)} %param.23) | copy-start | bytes 2692
  3.8 39.3 %copy-start.2 = (f32[7,16,16,128]{3,2,1,0:T(8,128)S(1)}, f32[7,16,16,128]{3,2,1,0:T(8,128)}, u32[]{:S(2)}) copy-start(f32[7,16,16,128]{3,2,1,0:T(8,128)} %now_ref.3) | copy-start | bytes 2752516
  3.8 39.3 %copy-start.4 = (f32[7,16,16,128]{3,2,1,0:T(8,128)S(1)}, f32[7,16,16,128]{3,2,1,0:T(8,128)}, u32[]{:S(2)}) copy-start(f32[7,16,16,128]{3,2,1,0:T(8,128)} %prev_ref.3) | copy-start | bytes 2752516
  10.2 9.0 %copy-start.9 = (bf16[64,64]{1,0:T(8,128)(2,1)S(1)}, bf16[64,64]{1,0:T(8,128)(2,1)}, u32[]{:S(2)}) copy-start(bf16[64,64]{1,0:T(8,128)(2,1)} %param.25) | copy-start | bytes 24580
  10.3 11.4 %collective-permute-start = (f32[576,128]{1,0:T(8,128)S(1)}, f32[576,128]{1,0:T(8,128)S(1)}, u32[]{:S(2)}, u32[]{:S(2)}) collective-permute-start(f32[576,128]{1,0:T(8,128)S(1)} %get-tuple-element.6), channel_id=1, source_target_pairs={{0,12},{12,24},{24,36},{36,48},{48,60},{60,72},{72,84},{84,96},{96... | collective-permute-start | bytes 884744 | tf_op jit(solution)/shard_map/ppermute | solution.py:464
  12.2 11.2 %collective-permute-start.1 = (f32[576,128]{1,0:T(8,128)S(1)}, f32[576,128]{1,0:T(8,128)S(1)}, u32[]{:S(2)}, u32[]{:S(2)}) collective-permute-start(f32[576,128]{1,0:T(8,128)S(1)} %get-tuple-element.7), channel_id=1, source_target_pairs={{12,0},{24,12},{36,24},{48,36},{60,48},{72,60},{84,72},{96,84},{10... | collective-permute-start | bytes 884744 | tf_op jit(solution)/shard_map/ppermute | solution.py:465
  19.4 0.8 copy-start.8
  20.3 0.7 copy-start.16
  23.5 12.4 %copy-start.17 = (f32[64]{0:T(128)S(1)}, f32[64]{0:T(128)}, u32[]{:S(2)}) copy-start(f32[64]{0:T(128)} %param.26) | copy-start | bytes 772
  23.5 13.5 %collective-permute-start.3 = (f32[344,128]{1,0:T(8,128)S(1)}, f32[344,128]{1,0:T(8,128)S(1)}, u32[]{:S(2)}, u32[]{:S(2)}) collective-permute-start(f32[344,128]{1,0:T(8,128)S(1)} %get-tuple-element.14), channel_id=1, source_target_pairs={{1,0},{2,1},{3,2},{4,3},{5,4},{6,5},{7,6},{8,7},{9,8},{10,9},{11,1... | collective-permute-start | bytes 528392 | tf_op jit(solution)/shard_map/ppermute | solution.py:479
  34.0 7.3 %collective-permute-start.2 = (f32[344,128]{1,0:T(8,128)S(1)}, f32[344,128]{1,0:T(8,128)S(1)}, u32[]{:S(2)}, u32[]{:S(2)}) collective-permute-start(f32[344,128]{1,0:T(8,128)S(1)} %get-tuple-element.15), channel_id=1, source_target_pairs={{0,1},{1,2},{2,3},{3,4},{4,5},{5,6},{6,7},{7,8},{8,9},{9,10},{10,1... | collective-permute-start | bytes 528392 | tf_op jit(solution)/shard_map/ppermute | solution.py:478
  41.3 0.7 copy-start.14
  42.0 0.7 copy-start.15
  42.9 0.7 copy-start.5
  43.0 0.7 copy-start.6
  43.0 0.7 copy-start.7

commit v2 on v1

v2 whole, which is shorter than its diff:
```python
import functools

import jax
import jax.numpy as jnp
from jax import lax
from jax.experimental import pallas as pl
from jax.experimental.pallas import tpu as pltpu
from jax.sharding import PartitionSpec as P

VARS = 7
LEV = 16
ROWS = 16
LANES = 128
POLAR = 4
NETWORK = True
NLEVELS = 16
PARTS = ((0, 112), (112, 112))
HID = 64
GPT = 224
LISTED = 1536
TILES_POLAR = VARS * LEV // 2
TILES_COLS = 16
LON_ROWS = 8 * (TILES_POLAR + TILES_COLS)
LAT_NOW = VARS * 4
LAT_PREV = VARS * 2
LAT_ROWS = 8 * (LAT_NOW + LAT_PREV + 1)
LOG2E = 1.4426950408889634
TAU_SCALE = 0.15

f32 = jnp.float32
bf16 = jnp.bfloat16


def iotas():
    lane = lax.broadcasted_iota(jnp.int32, (8, LANES), 1)
    sub = lax.broadcasted_iota(jnp.int32, (8, LANES), 0)
    return lane, sub


def roll_lanes(x, shift):
    return pltpu.roll(x, shift, 1)


def roll_subs(x, shift):
    return pltpu.roll(x, shift, 0)


def pick(x, index):
    return jnp.take_along_axis(x, index, axis=1, mode="promise_in_bounds")


def col_tile(which, half, group):
    return 8 * (TILES_POLAR + which * 8 + half * 4 + group)


def pack_kernel(
    first_ref, zc_ref, now_hbm, prev_hbm, east_ref, west_ref, north_ref, south_ref, now_ref, prev_ref, sems
):
    def fetch(k, which):
        src, dst = ((now_hbm, now_ref), (prev_hbm, prev_ref))[which]
        return pltpu.make_async_copy(src.at[:, k], dst.at[:, k], sems.at[which, k])

    def start(k, carry):
        for part in range(2):
            for which in range(2):
                fetch(k + 8 * part, which).start()
        return carry

    lax.fori_loop(0, 8, start, 0)
    lane, sub = iotas()
    first = first_ref[0]
    base = pl.multiple_of(jnp.where(first == 1, 0, 8), 8)
    turn = jnp.where(first == 1, 0, 4)
    extra = jnp.where(first == 1, 4, 11)

    def levels(k, tiles):
        for part in range(2):
            for which in range(2):
                fetch(k + 8 * part, which).wait()
        for v in range(VARS):
            both = []
            for ref in (now_ref, prev_ref):
                pair = [
                    roll_subs(ref[v, k + 8 * part, pl.ds(base, 8), :], (4 * part + turn) % 8)
                    for part in range(2)
                ]
                both.append(jnp.where(sub < 4, pair[0], pair[1]))
            tile, old = both[0], roll_lanes(both[1], 64)
            row = jnp.where(
                sub < 4,
                jnp.broadcast_to(now_ref[v, k, pl.ds(extra, 1), :], (8, LANES)),
                jnp.broadcast_to(now_ref[v, k + 8, pl.ds(extra, 1), :], (8, LANES)),
            )
            at = pl.multiple_of((v * 8 + k) * 8, 8)
            east_ref[pl.ds(at, 8), :] = jnp.where(
                lane >= 64, tile, jnp.where(lane >= 32, old, roll_lanes(row, 32))
            )
            west_ref[pl.ds(at, 8), :] = jnp.where(
                lane < 64, tile, jnp.where(lane < 96, old, roll_lanes(row, 96))
            )
        tiles = list(tiles)
        for part in range(2):
            for v in range(VARS):
                at = (v % 2) * 64 + 4 * (k + 8 * part)
                mine = (lane >= at) & (lane < at + 4)
                for which, ref in enumerate((now_ref, prev_ref)):
                    for half in range(2):
                        x = ref[v, k + 8 * part, 8 * half : 8 * half + 8, :]
                        slot = which * 8 + half * 4 + v // 2
                        tiles[slot] = jnp.where(mine, roll_lanes(x, at + 2), tiles[slot])
        return tuple(tiles)

    tiles = lax.fori_loop(0, 8, levels, (jnp.zeros((8, LANES), f32),) * TILES_COLS)
    for i in range(TILES_COLS):
        at = 8 * (TILES_POLAR + i)
        west_ref[at : at + 8, :] = tiles[i]
        east_ref[at : at + 8, :] = tiles[i]

    def rows_now(g, carry):
        for v in range(VARS):
            north = None
            south = None
            for h in range(4):
                up = now_ref[v, g + 4 * h, 0:8, :]
                down = now_ref[v, g + 4 * h, 8:16, :]
                up = roll_subs(up, 2 * h) if h else up
                down = roll_subs(down, (2 * h + 2) % 8) if h != 3 else down
                mask = sub >= 2 * h
                north = up if h == 0 else jnp.where(mask, up, north)
                south = down if h == 0 else jnp.where(mask, down, south)
            at = pl.multiple_of((v * 4 + g) * 8, 8)
            north_ref[pl.ds(at, 8), :] = north
            south_ref[pl.ds(at, 8), :] = south
        return carry

    lax.fori_loop(0, 4, rows_now, 0)

    def rows_prev(g, carry):
        for v in range(VARS):
            north = None
            south = None
            for h in range(8):
                up = prev_ref[v, g + 2 * h, 0:8, :]
                down = prev_ref[v, g + 2 * h, 8:16, :]
                up = roll_subs(up, h) if h else up
                down = roll_subs(down, h + 1) if h != 7 else down
                mask = sub >= h
                north = up if h == 0 else jnp.where(mask, up, north)
                south = down if h == 0 else jnp.where(mask, down, south)
            at = pl.multiple_of((LAT_NOW + v * 2 + g) * 8, 8)
            north_ref[pl.ds(at, 8), :] = north
            south_ref[pl.ds(at, 8), :] = south
        return carry

    lax.fori_loop(0, 2, rows_prev, 0)
    north_ref[LAT_ROWS - 8 :, :] = jnp.full((8, LANES), zc_ref[0], f32)
    south_ref[LAT_ROWS - 8 :, :] = jnp.full((8, LANES), zc_ref[ROWS - 1], f32)


def prep_kernel(
    lon_ref,
    stride_ref,
    flen_ref,
    zc_ref,
    count_ref,
    listed_ref,
    w1_ref,
    shift_out,
    cz_out,
    mask_out,
    w1_out,
):
    sub = lax.broadcasted_iota(jnp.int32, (ROWS, LANES), 0)
    tables = []
    for ref in (stride_ref, flen_ref, zc_ref):
        x = jnp.full((ROWS, LANES), ref[0])
        for j in range(1, ROWS):
            x = jnp.where(sub == j, ref[j], x)
        tables.append(x)
    shift_out[0:ROWS, :] = tables[0]
    shift_out[ROWS : 2 * ROWS, :] = tables[1]
    cz_out[...] = tables[2] * (1.0 / tables[0].astype(f32))

    listed = listed_ref[...]
    live = lax.broadcasted_iota(jnp.int32, (1, LISTED), 1) < count_ref[0, lon_ref[0]]
    row_hot = (listed // LANES == lax.broadcasted_iota(jnp.int32, (ROWS, LISTED), 0)) & live
    col_hot = listed % LANES == lax.broadcasted_iota(jnp.int32, (LANES, LISTED), 0)
    mask_out[...] = lax.dot_general(
        jnp.where(row_hot, 1.0, 0.0).astype(bf16),
        jnp.where(col_hot, 1.0, 0.0).astype(bf16),
        (((1,), (1,)), ((), ())),
        preferred_element_type=f32,
    )
    column = lax.broadcasted_iota(jnp.int32, (HID, VARS * ROWS), 1) % ROWS
    w1 = w1_ref[...]
    for r in range(ROWS):
        w1_out[r] = jnp.where(column == r, w1, 0.0).astype(bf16)


def main_kernel(
    first_ref,
    merid_ref,
    filter_ref,
    now_ref,
    prev_ref,
    fromwest_ref,
    fromeast_ref,
    fromnorth_ref,
    fromsouth_ref,
    shift_ref,
    cz_ref,
    mask_ref,
    w1_ref,
    b1_ref,
    w2_ref,
    b2_ref,
    w3_ref,
    b3_ref,
    start_ref,
    prev_out,
    now_out,
    outp_ref,
    outn_ref,
    feats_ref,
    pstar_ref,
    h2a_ref,
    h2b_ref,
    part_ref,
    sems,
    last_sem,
):
    lane, sub = iotas()
    first = first_ref[0]
    west_cols = (lane % 4) < 2
    for i in range(TILES_COLS):
        at = 8 * (TILES_POLAR + i)
        pstar_ref[8 * i : 8 * i + 8, :] = jnp.where(
            west_cols, fromwest_ref[at : at + 8, :], fromeast_ref[at : at + 8, :]
        )

    def outer(at):
        return jnp.where(
            sub == 7,
            jnp.broadcast_to(fromnorth_ref[at : at + 1, :], (8, LANES)),
            jnp.broadcast_to(fromsouth_ref[at : at + 1, :], (8, LANES)),
        )

    edge = (lane < 2) | (lane >= 126)

    def shifts(amount):
        return (
            (lane + amount) % LANES,
            lane < amount,
            (lane - amount) % LANES,
            lane >= LANES - amount,
        )

    def around(x, other, tab):
        if tab is None:
            return (
                roll_lanes(jnp.where(lane == 0, other, x), LANES - 1),
                roll_lanes(jnp.where(lane == LANES - 1, other, x), 1),
            )
        return (
            pick(jnp.where(tab[1], other, x), tab[0]),
            pick(jnp.where(tab[3], other, x), tab[2]),
        )

    def merid_of(t0, t1, t2, last):
        u0, u1, u2 = (roll_subs(t, 7) for t in (t0, t1, t2))
        d0, d1, d2 = (roll_subs(t, 1) for t in (t0, t1, t2))
        bottom = sub == 7
        top = sub == 0
        out = [
            jnp.where(bottom, u1, u0) - jnp.where(top, d2, d0),
            jnp.where(bottom, u2, u1) - jnp.where(top, d0, d1),
        ]
        if last:
            out.append(jnp.where(bottom, u0, u2) - jnp.where(top, d1, d2))
        return out

    def take_steps(polar):
        is_polar = (sub < 4) if polar == 0 else (sub >= 4)

        def level(k, carry):
            mc = merid_ref[k]
            fc = filter_ref[k]
            pol_at = 8 * (k % 8)
            pol_turn = (4 * polar + 8 - 4 * (k // 8)) % 8
            gn, hn = k % 4, k // 4
            gp, hp = k % 2, k // 2
            s_tab = shifts(shift_ref[8 * polar : 8 * polar + 8, :])
            m_tab = shifts(shift_ref[ROWS + 8 * polar : ROWS + 8 * polar + 8, :])
            cz = [cz_ref[0:8, :], cz_ref[8:16, :], outer(LAT_ROWS - 4)]

            def gather_tiles(v):
                group = v // 2
                back = 126 - (v % 2) * 64 - 4 * k
                cells = [now_ref[v, k, 0:8, :], now_ref[v, k, 8:16, :]]
                old = [prev_ref[v, k, 0:8, :], prev_ref[v, k, 8:16, :]]
                at = pl.multiple_of((v * 4 + gn) * 8, 8)
                t2 = jnp.where(
                    sub >= 4,
                    roll_subs(fromnorth_ref[pl.ds(at, 8), :], (14 - 2 * hn) % 8),
                    roll_subs(fromsouth_ref[pl.ds(at, 8), :], (8 - 2 * hn) % 8),
                )
                at = pl.multiple_of((LAT_NOW + v * 2 + gp) * 8, 8)
                t2_old = jnp.where(
                    sub >= 4,
                    roll_subs(fromnorth_ref[pl.ds(at, 8), :], 7 - hp),
                    roll_subs(fromsouth_ref[pl.ds(at, 8), :], (8 - hp) % 8),
                )
                at = pl.multiple_of(v * 64 + pol_at, 8)
                te = fromeast_ref[pl.ds(at, 8), :]
                tw = fromwest_ref[pl.ds(at, 8), :]
                natural = roll_subs(jnp.where(lane < 64, te, tw), pol_turn)
                crossed = roll_subs(jnp.where(lane < 64, tw, te), pol_turn)
                near = jnp.where(lane < 64, roll_lanes(crossed, 32), roll_lanes(crossed, 96))
                strip = jnp.where(is_polar, natural, roll_subs(near, 4))
                strip_old = roll_lanes(crossed, 64)
                halo = []
                halo_old = []
                for half in range(2):
                    tile = 8 * (half * 4 + group)
                    x = roll_lanes(pstar_ref[tile : tile + 8, :], back)
                    halo.append(jnp.where(edge, x, strip) if half == polar else x)
                    x = roll_lanes(pstar_ref[tile + 64 : tile + 72, :], back)
                    halo_old.append(jnp.where(edge, x, strip_old) if half == polar else x)
                t2_halo = roll_lanes(outer(LAT_ROWS - 8 + group), back)
                return cells, old, t2, t2_old, halo, halo_old, t2_halo

            def tend(x, other, merid, cu, cv, half):
                right, left = around(x, other, s_tab if half == polar else None)
                zonal = right - left
                if half == polar:
                    right, left = around(x, other, m_tab)
                return fc * (right + left - 2.0 * x) - cu * zonal - cv * merid

            def first_step(tile, cu_c, cv_c, cu_h, cv_h):
                cells, old, t2, t2_old, halo, halo_old, t2_halo = tile
                md = merid_of(cells[0], cells[1], t2, True)
                mh = merid_of(halo[0], halo[1], t2_halo, False)
                new = []
                new_halo = []
                filtered = []
                for h in range(2):
                    x, o = cells[h], halo[h]
                    n = old[h] + tend(x, o, md[h], cu_c[h], cv_c[h], h)
                    new.append(n)
                    filtered.append(x + 0.1 * (old[h] - 2.0 * x + n))
                    new_halo.append(halo_old[h] + tend(o, x, mh[h], cu_h[h], cv_h[h], h))
                new_t2 = t2_old + tend(t2, t2_halo, md[2], cu_c[2], cv_c[2], 2)
                return new, new_halo, new_t2, filtered

            def second_step(v, stepped, cu, cv):
                new, new_halo, new_t2, filtered = stepped
                md = merid_of(new[0], new[1], new_t2, False)
                both = []
                for h in range(2):
                    x = new[h]
                    n = filtered[h] + tend(x, new_halo[h], md[h], cu[h], cv[h], h)
                    outn_ref[v, k, 8 * h : 8 * h + 8, :] = n
                    outp_ref[v, k, 8 * h : 8 * h + 8, :] = x + 0.1 * (filtered[h] - 2.0 * x + n)
                    both.append(n)
                at = pl.multiple_of((k % 2) * LANES, LANES)
                feats_ref[k // 2, 16 * v : 16 * v + 16, pl.ds(at, LANES)] = jnp.concatenate(
                    both, axis=0
                ).astype(bf16)

            u = gather_tiles(0)
            w = gather_tiles(1)
            cu_c = [cz[h] * u[0][h] for h in range(2)] + [cz[2] * u[2]]
            cv_c = [mc * w[0][h] for h in range(2)] + [mc * w[2]]
            cu_h = [cz[h] * u[4][h] for h in range(2)]
            cv_h = [mc * w[4][h] for h in range(2)]
            stepped_u = first_step(u, cu_c, cv_c, cu_h, cv_h)
            stepped_w = first_step(w, cu_c, cv_c, cu_h, cv_h)
            cu = [cz[h] * stepped_u[0][h] for h in range(2)]
            cv = [mc * stepped_w[0][h] for h in range(2)]
            second_step(0, stepped_u, cu, cv)
            second_step(1, stepped_w, cu, cv)
            for v in range(2, VARS):
                second_step(v, first_step(gather_tiles(v), cu_c, cv_c, cu_h, cv_h), cu, cv)
            pltpu.make_async_copy(outp_ref.at[:, k], prev_out.at[:, k], sems.at[k, 0]).start()
            pltpu.make_async_copy(outn_ref.at[0:2, k], now_out.at[0:2, k], sems.at[k, 1]).start()
            pltpu.make_async_copy(outn_ref.at[3:7, k], now_out.at[3:7, k], sems.at[k, 2]).start()
            return carry

        lax.fori_loop(0, NLEVELS, level, 0)

    @pl.when(first == 1)
    def _():
        take_steps(0)

    @pl.when(first != 1)
    def _():
        take_steps(1)

    start_sum = None
    for i in range(GPT // 8):
        t = jnp.exp2(-TAU_SCALE * start_ref[8 * i : 8 * i + 8, :])
        start_sum = t if start_sum is None else start_sum + t

    def hidden(r, p, dst):
        z = jnp.dot(w1_ref[r], feats_ref[p], preferred_element_type=f32)
        z = z + jnp.concatenate([b1_ref[...]] * 2, axis=1)
        h1 = (z * jnp.tanh(z) + z).astype(bf16)
        z = jnp.dot(w2_ref[...], h1, preferred_element_type=f32)
        z = z + jnp.concatenate([b2_ref[...]] * 2, axis=1)
        dst[p] = (z * jnp.tanh(z) + z).astype(bf16)

    def optics(at, width, p, src, total):
        y = jnp.dot(w3_ref[at : at + width, :], src[p], preferred_element_type=f32)
        for side in range(2):
            x = y[:, LANES * side : LANES * side + LANES] * LOG2E + b3_ref[at : at + width, :]
            e = jnp.exp2(jnp.minimum(x, 126.0))
            total = total + jnp.maximum(x, jnp.log2(1.0 + e))
            t = jnp.exp2(-TAU_SCALE * total)
            s = t[0:8]
            for i in range(1, width // 8):
                s = s + t[8 * i : 8 * i + 8]
            k = 2 * p + side
            part_ref[k] = s if at == 0 else part_ref[k] + s
        return total

    def phase(r, src, after, dst):
        done = 0
        turns = len(PARTS) * (LEV // 2)
        for n, (at, width) in enumerate(PARTS):
            total = start_ref[at : at + width, :]
            for p in range(LEV // 2):
                while done * turns < (LEV // 2) * (n * (LEV // 2) + p + 1):
                    hidden(after, done, dst)
                    done += 1
                total = optics(at, width, p, src, total)
        lit = mask_ref[pl.ds(r, 1), :] > 0.5
        before = start_sum
        for k in range(LEV):
            now = part_ref[k]
            heat = jnp.sum(before - now, axis=0, keepdims=True)
            before = now
            outn_ref[2, k, pl.ds(r, 1), :] = outn_ref[2, k, pl.ds(r, 1), :] + jnp.where(
                lit, heat, 0.0
            )

    def two_rows(i, carry):
        phase(2 * i, h2a_ref, 2 * i + 1, h2b_ref)
        phase(2 * i + 1, h2b_ref, jnp.minimum(2 * i + 2, ROWS - 1), h2a_ref)
        return carry

    for p in range(LEV // 2):
        hidden(0, p, h2a_ref)
    lax.fori_loop(0, ROWS // 2 if NETWORK else 0, two_rows, 0)
    last = pltpu.make_async_copy(outn_ref.at[2], now_out.at[2], last_sem)
    last.start()

    def drain(k, carry):
        pltpu.make_async_copy(outp_ref.at[:, k], prev_out.at[:, k], sems.at[k, 0]).wait()
        pltpu.make_async_copy(outn_ref.at[0:2, k], now_out.at[0:2, k], sems.at[k, 1]).wait()
        pltpu.make_async_copy(outn_ref.at[3:7, k], now_out.at[3:7, k], sems.at[k, 2]).wait()
        return carry

    lax.fori_loop(0, NLEVELS, drain, 0)
    last.wait()


VMEM = pl.BlockSpec(memory_space=pltpu.VMEM)
SMEM = pl.BlockSpec(memory_space=pltpu.SMEM)
ANY = pl.BlockSpec(memory_space=pl.ANY)
HBM = pl.BlockSpec(memory_space=pltpu.HBM)


def body(
    state_prev,
    state_now,
    stride_table,
    filter_len,
    zonal_coef,
    merid_coef,
    filter_coef,
    w_first,
    b_first,
    w_second,
    b_second,
    w_third,
    b_third,
    band_weight,
    sunlit_cols,
    sunlit_count,
):
    first = (lax.axis_index("lat") == 0).astype(jnp.int32).reshape(1)
    lon = lax.axis_index("lon").astype(jnp.int32).reshape(1)

    lon_shape = jax.ShapeDtypeStruct((LON_ROWS, LANES), f32)
    lat_shape = jax.ShapeDtypeStruct((LAT_ROWS, LANES), f32)
    state = jax.ShapeDtypeStruct(state_now.shape, f32)
    east, west, north, south = pl.pallas_call(
        pack_kernel,
        name="pack",
        out_shape=(lon_shape, lon_shape, lat_shape, lat_shape),
        in_specs=[SMEM, SMEM, HBM, HBM],
        out_specs=(VMEM,) * 4,
        scratch_shapes=[
            pltpu.VMEM(state_now.shape, f32),
            pltpu.VMEM(state_now.shape, f32),
            pltpu.SemaphoreType.DMA((2, LEV)),
        ],
        compiler_params=pltpu.CompilerParams(vmem_limit_bytes=16 << 20),
    )(first, zonal_coef, state_now, state_prev)

    def wide(vector):
        return jnp.broadcast_to(vector[:, None], (vector.shape[0], LANES))

    w1 = jnp.repeat(w_first.T.astype(f32) * 0.5, ROWS, axis=1)
    shift, cz, mask, w1 = pl.pallas_call(
        prep_kernel,
        name="prep",
        out_shape=(
            jax.ShapeDtypeStruct((2 * ROWS, LANES), jnp.int32),
            jax.ShapeDtypeStruct((ROWS, LANES), f32),
            jax.ShapeDtypeStruct((ROWS, LANES), f32),
            jax.ShapeDtypeStruct((ROWS, HID, VARS * ROWS), bf16),
        ),
        in_specs=[SMEM] * 5 + [VMEM] * 2,
        out_specs=(VMEM,) * 4,
        compiler_params=pltpu.CompilerParams(vmem_limit_bytes=8 << 20),
    )(lon, stride_table, filter_len, zonal_coef, sunlit_count, sunlit_cols.reshape(1, LISTED), w1)
    w2 = (w_second.T.astype(f32) * 0.5).astype(bf16)
    w3 = w_third.T
    b1 = wide(b_first * 0.5)
    b2 = wide(b_second * 0.5)
    b3 = wide(b_third * LOG2E)
    start = wide(jnp.log2(band_weight) * (-1.0 / TAU_SCALE))

    nlon = lax.axis_size("lon")
    nlat = lax.axis_size("lat")
    fromwest = lax.ppermute(east, "lon", [(i, (i + 1) % nlon) for i in range(nlon)])
    fromeast = lax.ppermute(west, "lon", [((i + 1) % nlon, i) for i in range(nlon)])

    west_cols = (jnp.arange(LANES) % 4 < 2)[None, :]

    def corners(half, row):
        at = col_tile(0, half, 0)
        pieces = [
            x[at : at + 32].reshape(4, 8, LANES)[:, row] for x in (fromwest, fromeast)
        ]
        return jnp.where(west_cols, pieces[0], pieces[1])

    north = lax.dynamic_update_slice(north, corners(0, 0), (LAT_ROWS - 8, 0))
    south = lax.dynamic_update_slice(south, corners(1, 7), (LAT_ROWS - 8, 0))
    (north, south, shift, cz, mask, w1, w2, w3, b1, b2, b3, start) = lax.optimization_barrier(
        (north, south, shift, cz, mask, w1, w2, w3, b1, b2, b3, start)
    )
    fromnorth = lax.ppermute(south, "lat", [(i, i + 1) for i in range(nlat - 1)])
    fromsouth = lax.ppermute(north, "lat", [(i + 1, i) for i in range(nlat - 1)])

    prev_out, now_out = pl.pallas_call(
        main_kernel,
        name="main",
        out_shape=(state, state),
        in_specs=[SMEM] * 3 + [VMEM] * 16,
        out_specs=(ANY, ANY),
        scratch_shapes=[
            pltpu.VMEM(state_now.shape, f32),
            pltpu.VMEM(state_now.shape, f32),
            pltpu.VMEM((LEV // 2, VARS * ROWS, 2 * LANES), bf16),
            pltpu.VMEM((8 * TILES_COLS, LANES), f32),
            pltpu.VMEM((LEV // 2, HID, 2 * LANES), bf16),
            pltpu.VMEM((LEV // 2, HID, 2 * LANES), bf16),
            pltpu.VMEM((LEV, 8, LANES), f32),
            pltpu.SemaphoreType.DMA((LEV, 3)),
            pltpu.SemaphoreType.DMA,
        ],
        compiler_params=pltpu.CompilerParams(vmem_limit_bytes=36 << 20),
    )(
        first,
        merid_coef,
        filter_coef,
        state_now,
        state_prev,
        fromwest,
        fromeast,
        fromnorth,
        fromsouth,
        shift,
        cz,
        mask,
        w1,
        b1,
        w2,
        b2,
        w3,
        b3,
        start,
    )
    return prev_out, now_out


def solution(mesh):
    in_specs = (
        P(None, None, "lat", "lon"),
        P(None, None, "lat", "lon"),
        P("lat"),
        P("lat"),
        P("lat"),
        P(),
        P(),
        P(),
        P(),
        P(),
        P(),
        P(),
        P(),
        P(),
        P("lat", "lon", None),
        P("lat", None),
    )
    out_specs = (P(None, None, "lat", "lon"), P(None, None, "lat", "lon"))
    return jax.shard_map(body, mesh=mesh, in_specs=in_specs, out_specs=out_specs, check_vma=False)
```

time: 78.7 us -> 67.4 us (0.86)
  the two profiles are of different devices: /device:TPU:64 before, /device:TPU:63 now
where the time goes in v2:
time: 67.4 us; the launch traced here: 66.9 us
  Pallas kernels  33.8 us (50%)
  starting transfers between devices  15.5 us (23%)
  waiting for transfers between devices  11.6 us (17%)
  local copies, waits for them, and re-layouts  5.03 us (7%)
  between operations  0.96 us (1%)
    pallas_call x1, Pallas kernels, body(): pl.pallas_call(main_kernel, name='main', out_shape=(state, state), in_spe...  30.3 us
    ppermute x1, starting transfers between devices, body(): lax.ppermute(east, 'lon', [(i, (i + 1) % nlon) for i in range(nlon)])  10.9 us
    ppermute x1, waiting for transfers between devices, body(): lax.ppermute(west, 'lon', [((i + 1) % nlon, i) for i in range(nlon)])  6.69 us
    unnamed x38, local copies, waits for them, and re-layouts  4.61 us
    ppermute x1, waiting for transfers between devices, body(): lax.ppermute(north, 'lat', [(i + 1, i) for i in range(nlat - 1)])  3.83 us
    pallas_call x1, Pallas kernels, body(): pl.pallas_call(pack_kernel, name='pack', out_shape=(lon_shape, lon_shape,...  2.65 us
    ppermute x1, starting transfers between devices, body(): lax.ppermute(west, 'lon', [((i + 1) % nlon, i) for i in range(nlon)])  1.92 us
    ppermute x1, starting transfers between devices, body(): lax.ppermute(south, 'lat', [(i, i + 1) for i in range(nlat - 1)])  1.43 us
  transfers between devices with their start and end apart: 4, of which 3 were waited for; matrix products, arithmetic and copies ran while one was open for 0% of the time, Pallas kernels for 1%

profile of v2, /device:TPU:63, one launch (start us, length us, event | category | flops | bytes accessed | tf_op | source)
XLA Modules:
  0.0 66.9 jit_solution(17523135684936266599)
XLA Ops:
  0.7 0.6 copy-done.5
  1.3 1.2 %copy-done = f32[7,16,16,128]{3,2,1,0:T(8,128)S(1)} copy-done((f32[7,16,16,128]{3,2,1,0:T(8,128)S(1)}, f32[7,16,16,128]{3,2,1,0:T(8,128)}, u32[]{:S(2)}) %copy-start) | copy-done | bytes 917528
  2.5 1.2 %copy-done.2 = f32[7,16,16,128]{3,2,1,0:T(8,128)S(1)} copy-done((f32[7,16,16,128]{3,2,1,0:T(8,128)S(1)}, f32[7,16,16,128]{3,2,1,0:T(8,128)}, u32[]{:S(2)}) %copy-start.2) | copy-done | bytes 917528
  3.7 2.7 %pack.1 = (f32[576,128]{1,0:T(8,128)S(1)}, f32[576,128]{1,0:T(8,128)S(1)}, f32[344,128]{1,0:T(8,128)S(1)}, f32[344,128]{1,0:T(8,128)S(1)}) custom-call(s32[1]{0:T(128)} %bitcast.first_ref, f32[16]{0:T(128)S(1)} %copy-done.5, f32[7,16,16,128]{3,2,1,0:T(8,128)S(1)} %copy-done, f32[7,16,16,128]{3,2,1,0:T(8,128)S(1)} %copy-done.2), custom_call_target="tpu_custom_call" | custom-call | tf_op jit(solution)/shard_map/pack/pallas_call | solution.py:497
  6.4 0.0 copy-start.12
  6.4 10.9 %collective-permute-start = (f32[576,128]{1,0:T(8,128)S(1)}, f32[576,128]{1,0:T(8,128)S(1)}, u32[]{:S(2)}, u32[]{:S(2)}) collective-permute-start(f32[576,128]{1,0:T(8,128)S(1)} %get-tuple-element.22), channel_id=1, source_target_pairs={{0,12},{12,24},{24,36},{36,48},{48,60},{60,72},{72,84},{84,96},{96... | collective-permute-start | bytes 884744 | tf_op jit(solution)/shard_map/ppermute | solution.py:537
  17.2 1.9 %collective-permute-start.1 = (f32[576,128]{1,0:T(8,128)S(1)}, f32[576,128]{1,0:T(8,128)S(1)}, u32[]{:S(2)}, u32[]{:S(2)}) collective-permute-start(f32[576,128]{1,0:T(8,128)S(1)} %get-tuple-element.23), channel_id=1, source_target_pairs={{12,0},{24,12},{36,24},{48,36},{60,48},{72,60},{84,72},{96,84},{10... | collective-permute-start | bytes 884744 | tf_op jit(solution)/shard_map/ppermute | solution.py:538
  19.3 0.1 copy.26
  19.4 0.0 copy-start.11
  19.4 0.1 copy.25.w1_ref
  19.5 0.7 %copy-done.11 = bf16[64,224]{1,0:T(8,128)(2,1)S(1)} copy-done((bf16[64,224]{1,0:T(8,128)(2,1)S(1)}, bf16[64,224]{1,0:T(8,128)(2,1)}, u32[]{:S(2)}) %copy-start.11) | copy-done | bytes 28696
  20.1 0.1 copy.27
  20.3 0.0 copy-start.6
  20.3 0.0 copy-start.7
  20.3 0.0 copy-start.8
  20.3 0.5 copy-done.4
  20.8 0.1 copy-done.6
  20.9 0.0 copy-done.7
  20.9 0.0 copy-done.8
  21.0 0.9 %prep.1 = (s32[32,128]{1,0:T(8,128)S(1)}, f32[16,128]{1,0:T(8,128)S(1)}, f32[16,128]{1,0:T(8,128)S(1)}, bf16[16,64,112]{2,1,0:T(8,128)(2,1)S(1)}) custom-call(s32[1]{0:T(128)} %bitcast.9.lon_ref, s32[16]{0:T(128)S(1)} %copy-done.6, s32[16]{0:T(128)S(1)} %copy-done.7, f32[16]{0:T(128)S(1)} %copy-done.5, s32[1,64]{1,0:T(1,128)S(1)} %copy-done.8, ...), custom_call_target="tpu_custom_call" | custom-call | tf_op jit(solution)/shard_map/prep/pallas_call | solution.py:515
  21.9 6.7 %collective-permute-done.1.fromeast_ref = f32[576,128]{1,0:T(8,128)S(1)} collective-permute-done((f32[576,128]{1,0:T(8,128)S(1)}, f32[576,128]{1,0:T(8,128)S(1)}, u32[]{:S(2)}, u32[]{:S(2)}) %collective-permute-start.1) | collective-permute-done | bytes 294944 | tf_op jit(solution)/shard_map/ppermute | solution.py:538
  28.6 0.1 broadcast_in_dim.44.b2_ref
  28.7 0.1 broadcast_in_dim.43.b1_ref
  28.8 0.1 broadcast_in_dim.46.start_ref
  28.9 0.1 broadcast_in_dim.45.b3_ref
  29.0 0.0 copy-start.9
  29.0 0.0 copy-start.10
  29.0 1.4 %collective-permute-start.2 = (f32[344,128]{1,0:T(8,128)S(1)}, f32[344,128]{1,0:T(8,128)S(1)}, u32[]{:S(2)}, u32[]{:S(2)}) collective-permute-start(f32[344,128]{1,0:T(8,128)S(1)} %get-tuple-element.30), channel_id=1, source_target_pairs={{0,1},{1,2},{2,3},{3,4},{4,5},{5,6},{6,7},{7,8},{8,9},{9,10},{10,1... | collective-permute-start | bytes 528392 | tf_op jit(solution)/shard_map/ppermute | solution.py:554
  30.4 1.3 %collective-permute-start.3 = (f32[344,128]{1,0:T(8,128)S(1)}, f32[344,128]{1,0:T(8,128)S(1)}, u32[]{:S(2)}, u32[]{:S(2)}) collective-permute-start(f32[344,128]{1,0:T(8,128)S(1)} %get-tuple-element.31), channel_id=1, source_target_pairs={{1,0},{2,1},{3,2},{4,3},{5,4},{6,5},{7,6},{8,7},{9,8},{10,9},{11,1... | collective-permute-start | bytes 528392 | tf_op jit(solution)/shard_map/ppermute | solution.py:555
  31.7 1.1 %collective-permute-done.2.fromnorth_ref = f32[344,128]{1,0:T(8,128)S(1)} collective-permute-done((f32[344,128]{1,0:T(8,128)S(1)}, f32[344,128]{1,0:T(8,128)S(1)}, u32[]{:S(2)}, u32[]{:S(2)}) %collective-permute-start.2) | collective-permute-done | bytes 176160 | tf_op jit(solution)/shard_map/ppermute | solution.py:554
  32.8 3.8 %collective-permute-done.3.fromsouth_ref = f32[344,128]{1,0:T(8,128)S(1)} collective-permute-done((f32[344,128]{1,0:T(8,128)S(1)}, f32[344,128]{1,0:T(8,128)S(1)}, u32[]{:S(2)}, u32[]{:S(2)}) %collective-permute-start.3) | collective-permute-done | bytes 176160 | tf_op jit(solution)/shard_map/ppermute | solution.py:555
  36.6 30.3 %main.1 = (f32[7,16,16,128]{3,2,1,0:T(8,128)}, f32[7,16,16,128]{3,2,1,0:T(8,128)}) custom-call(s32[1]{0:T(128)} %bitcast.first_ref, f32[16]{0:T(128)S(1)} %copy-done.9, f32[16]{0:T(128)S(1)} %copy-done.10, f32[7,16,16,128]{3,2,1,0:T(8,128)S(1)} %copy-done.1, f32[7,16,16,128]{3,2,1,0:T(8,128)S(1)} %copy-done.3, ...), custom_call_target="tpu_custom_call" | custom-call | tf_op jit(solution)/shard_map/main/pallas_call | solution.py:557
  (37 shorter events, 0.1 us)
Async XLA Ops:
  0.6 0.7 copy-start.5
  1.3 1.2 %copy-start = (f32[7,16,16,128]{3,2,1,0:T(8,128)S(1)}, f32[7,16,16,128]{3,2,1,0:T(8,128)}, u32[]{:S(2)}) copy-start(f32[7,16,16,128]{3,2,1,0:T(8,128)} %now_ref.1) | copy-start | bytes 2752516
  2.5 1.2 %copy-start.2 = (f32[7,16,16,128]{3,2,1,0:T(8,128)S(1)}, f32[7,16,16,128]{3,2,1,0:T(8,128)}, u32[]{:S(2)}) copy-start(f32[7,16,16,128]{3,2,1,0:T(8,128)} %prev_ref.1) | copy-start | bytes 2752516
  3.7 15.5 %copy-start.16 = (f32[64]{0:T(128)S(1)}, f32[64]{0:T(128)}, u32[]{:S(2)}) copy-start(f32[64]{0:T(128)} %param.24) | copy-start | bytes 772
  3.7 15.5 %copy-start.14 = (f32[224]{0:T(256)S(1)}, f32[224]{0:T(256)}, u32[]{:S(2)}) copy-start(f32[224]{0:T(256)} %param.28) | copy-start | bytes 2692
  3.7 15.5 %copy-start.15 = (f32[224]{0:T(256)S(1)}, f32[224]{0:T(256)}, u32[]{:S(2)}) copy-start(f32[224]{0:T(256)} %param.29) | copy-start | bytes 2692
  3.7 15.6 %copy-start.13 = (bf16[7,64]{1,0:T(8,128)(2,1)S(1)}, bf16[7,64]{1,0:T(8,128)(2,1)}, u32[]{:S(2)}) copy-start(bf16[7,64]{1,0:T(8,128)(2,1)} %param.23) | copy-start | bytes 2692
  3.7 33.0 %copy-start.1 = (f32[7,16,16,128]{3,2,1,0:T(8,128)S(1)}, f32[7,16,16,128]{3,2,1,0:T(8,128)}, u32[]{:S(2)}) copy-start(f32[7,16,16,128]{3,2,1,0:T(8,128)} %now_ref.1) | copy-start | bytes 2752516
  3.7 33.0 %copy-start.3 = (f32[7,16,16,128]{3,2,1,0:T(8,128)S(1)}, f32[7,16,16,128]{3,2,1,0:T(8,128)}, u32[]{:S(2)}) copy-start(f32[7,16,16,128]{3,2,1,0:T(8,128)} %prev_ref.1) | copy-start | bytes 2752516
  6.4 12.9 %copy-start.12 = (bf16[64,64]{1,0:T(8,128)(2,1)S(1)}, bf16[64,64]{1,0:T(8,128)(2,1)}, u32[]{:S(2)}) copy-start(bf16[64,64]{1,0:T(8,128)(2,1)} %param.25) | copy-start | bytes 24580
  6.4 15.5 %collective-permute-start = (f32[576,128]{1,0:T(8,128)S(1)}, f32[576,128]{1,0:T(8,128)S(1)}, u32[]{:S(2)}, u32[]{:S(2)}) collective-permute-start(f32[576,128]{1,0:T(8,128)S(1)} %get-tuple-element.22), channel_id=1, source_target_pairs={{0,12},{12,24},{24,36},{36,48},{48,60},{60,72},{72,84},{84,96},{96... | collective-permute-start | bytes 884744 | tf_op jit(solution)/shard_map/ppermute | solution.py:537
  17.2 11.4 %collective-permute-start.1 = (f32[576,128]{1,0:T(8,128)S(1)}, f32[576,128]{1,0:T(8,128)S(1)}, u32[]{:S(2)}, u32[]{:S(2)}) collective-permute-start(f32[576,128]{1,0:T(8,128)S(1)} %get-tuple-element.23), channel_id=1, source_target_pairs={{12,0},{24,12},{36,24},{48,36},{60,48},{72,60},{84,72},{96,84},{10... | collective-permute-start | bytes 884744 | tf_op jit(solution)/shard_map/ppermute | solution.py:538
  19.4 0.8 %copy-start.11 = (bf16[64,224]{1,0:T(8,128)(2,1)S(1)}, bf16[64,224]{1,0:T(8,128)(2,1)}, u32[]{:S(2)}) copy-start(bf16[64,224]{1,0:T(8,128)(2,1)} %param.27) | copy-start | bytes 86020
  20.1 0.7 %copy-start.4 = (s32[1,1,1536]{2,1,0:T(1,128)S(1)}, s32[1,1,1536]{2,1,0:T(1,128)}, u32[]{:S(2)}) copy-start(s32[1,1,1536]{2,1,0:T(1,128)} %param.30) | copy-start | bytes 18436
  20.3 0.7 copy-start.6
  20.3 0.7 %copy-start.7 = (s32[16]{0:T(128)S(1)}, s32[16]{0:T(128)}, u32[]{:S(2)}) copy-start(s32[16]{0:T(128)} %flen_ref.1) | copy-start | bytes 196
  20.3 0.7 %copy-start.8 = (s32[1,64]{1,0:T(1,128)S(1)}, s32[1,64]{1,0:T(1,128)}, u32[]{:S(2)}) copy-start(s32[1,64]{1,0:T(1,128)} %count_ref.1) | copy-start | bytes 772
  20.9 0.9 %copy-start.17 = (f32[64]{0:T(128)S(1)}, f32[64]{0:T(128)}, u32[]{:S(2)}) copy-start(f32[64]{0:T(128)} %param.26) | copy-start | bytes 772
  29.0 7.7 %copy-start.9 = (f32[16]{0:T(128)S(1)}, f32[16]{0:T(128)}, u32[]{:S(2)}) copy-start(f32[16]{0:T(128)} %merid_ref.1) | copy-start | bytes 196
  29.0 7.7 %copy-start.10 = (f32[16]{0:T(128)S(1)}, f32[16]{0:T(128)}, u32[]{:S(2)}) copy-start(f32[16]{0:T(128)} %filter_ref.1) | copy-start | bytes 196
  29.0 3.8 %collective-permute-start.2 = (f32[344,128]{1,0:T(8,128)S(1)}, f32[344,128]{1,0:T(8,128)S(1)}, u32[]{:S(2)}, u32[]{:S(2)}) collective-permute-start(f32[344,128]{1,0:T(8,128)S(1)} %get-tuple-element.30), channel_id=1, source_target_pairs={{0,1},{1,2},{2,3},{3,4},{4,5},{5,6},{6,7},{7,8},{8,9},{9,10},{10,1... | collective-permute-start | bytes 528392 | tf_op jit(solution)/shard_map/ppermute | solution.py:554
  30.4 6.2 %collective-permute-start.3 = (f32[344,128]{1,0:T(8,128)S(1)}, f32[344,128]{1,0:T(8,128)S(1)}, u32[]{:S(2)}, u32[]{:S(2)}) collective-permute-start(f32[344,128]{1,0:T(8,128)S(1)} %get-tuple-element.31), channel_id=1, source_target_pairs={{1,0},{2,1},{3,2},{4,3},{5,4},{6,5},{7,6},{8,7},{9,8},{10,9},{11,1... | collective-permute-start | bytes 528392 | tf_op jit(solution)/shard_map/ppermute | solution.py:555

commit v3 on v2

--- a/solution.py
+++ b/solution.py
@@ -13,6 +13,8 @@
 LANES = 128
 POLAR = 4
 NETWORK = True
+STEPLIM = 8
+MAINLIM = 16
 NLEVELS = 16
 PARTS = ((0, 112), (112, 112))
 HID = 64
@@ -54,7 +56,18 @@
 
 
 def pack_kernel(
-    first_ref, zc_ref, now_hbm, prev_hbm, east_ref, west_ref, north_ref, south_ref, now_ref, prev_ref, sems
+    first_ref,
+    even_ref,
+    zc_ref,
+    now_hbm,
+    prev_hbm,
+    east_ref,
+    west_ref,
+    lata_ref,
+    latb_ref,
+    now_ref,
+    prev_ref,
+    sems,
 ):
     def fetch(k, which):
         src, dst = ((now_hbm, now_ref), (prev_hbm, prev_ref))[which]
@@ -69,6 +82,12 @@
     lax.fori_loop(0, 8, start, 0)
     lane, sub = iotas()
     first = first_ref[0]
+    even = even_ref[0] == 1
+
+    def put(at, north, south):
+        lata_ref[pl.ds(at, 8), :] = jnp.where(even, south, north)
+        latb_ref[pl.ds(at, 8), :] = jnp.where(even, north, south)
+
     base = pl.multiple_of(jnp.where(first == 1, 0, 8), 8)
     turn = jnp.where(first == 1, 0, 4)
     extra = jnp.where(first == 1, 4, 11)
@@ -129,8 +148,7 @@
                 north = up if h == 0 else jnp.where(mask, up, north)
                 south = down if h == 0 else jnp.where(mask, down, south)
             at = pl.multiple_of((v * 4 + g) * 8, 8)
-            north_ref[pl.ds(at, 8), :] = north
-            south_ref[pl.ds(at, 8), :] = south
+            put(at, north, south)
         return carry
 
     lax.fori_loop(0, 4, rows_now, 0)
@@ -148,13 +166,15 @@
                 north = up if h == 0 else jnp.where(mask, up, north)
                 south = down if h == 0 else jnp.where(mask, down, south)
             at = pl.multiple_of((LAT_NOW + v * 2 + g) * 8, 8)
-            north_ref[pl.ds(at, 8), :] = north
-            south_ref[pl.ds(at, 8), :] = south
+            put(at, north, south)
         return carry
 
     lax.fori_loop(0, 2, rows_prev, 0)
-    north_ref[LAT_ROWS - 8 :, :] = jnp.full((8, LANES), zc_ref[0], f32)
-    south_ref[LAT_ROWS - 8 :, :] = jnp.full((8, LANES), zc_ref[ROWS - 1], f32)
+    put(
+        LAT_ROWS - 8,
+        jnp.full((8, LANES), zc_ref[0], f32),
+        jnp.full((8, LANES), zc_ref[ROWS - 1], f32),
+    )
 
 
 def prep_kernel(
@@ -197,7 +217,55 @@
         w1_out[r] = jnp.where(column == r, w1, 0.0).astype(bf16)
 
 
-def main_kernel(
+def shifts(amount):
+    lane, _ = iotas()
+    return (
+        (lane + amount) % LANES,
+        lane < amount,
+        (lane - amount) % LANES,
+        lane >= LANES - amount,
+    )
+
+
+def around(x, other, tab):
+    lane, _ = iotas()
+    if tab is None:
+        return (
+            roll_lanes(jnp.where(lane == 0, other, x), LANES - 1),
+            roll_lanes(jnp.where(lane == LANES - 1, other, x), 1),
+        )
+    return (
+        pick(jnp.where(tab[1], other, x), tab[0]),
+        pick(jnp.where(tab[3], other, x), tab[2]),
+    )
+
+
+def merid_of(t0, t1, above, below):
+    _, sub = iotas()
+    u0, u1, d0, d1 = roll_subs(t0, 7), roll_subs(t1, 7), roll_subs(t0, 1), roll_subs(t1, 1)
+    bottom = sub == 7
+    top = sub == 0
+    return (
+        jnp.where(bottom, u1, u0) - jnp.where(top, above, d0),
+        jnp.where(bottom, below, u1) - jnp.where(top, d0, d1),
+    )
+
+
+def tend(x, other, merid, cu, cv, fc, s_tab, m_tab):
+    right, left = around(x, other, s_tab)
+    zonal = right - left
+    if m_tab is not None:
+        right, left = around(x, other, m_tab)
+    return fc * (right + left - 2.0 * x) - cu * zonal - cv * merid
+
+
+def tables_of(shift_ref, polar):
+    s_tab = shifts(shift_ref[8 * polar : 8 * polar + 8, :])
+    m_tab = shifts(shift_ref[ROWS + 8 * polar : ROWS + 8 * polar + 8, :])
+    return [(s_tab, m_tab) if h == polar else (None, None) for h in range(2)]
+
+
+def step_kernel(
     first_ref,
     merid_ref,
     filter_ref,
@@ -205,29 +273,13 @@
     prev_ref,
     fromwest_ref,
     fromeast_ref,
-    fromnorth_ref,
-    fromsouth_ref,
     shift_ref,
     cz_ref,
-    mask_ref,
-    w1_ref,
-    b1_ref,
-    w2_ref,
-    b2_ref,
-    w3_ref,
-    b3_ref,
-    start_ref,
-    prev_out,
-    now_out,
-    outp_ref,
-    outn_ref,
-    feats_ref,
+    new_ref,
+    halo_ref,
+    filtered_ref,
+    wind_ref,
     pstar_ref,
-    h2a_ref,
-    h2b_ref,
-    part_ref,
-    sems,
-    last_sem,
 ):
     lane, sub = iotas()
     first = first_ref[0]
@@ -237,49 +289,10 @@
         pstar_ref[8 * i : 8 * i + 8, :] = jnp.where(
             west_cols, fromwest_ref[at : at + 8, :], fromeast_ref[at : at + 8, :]
         )
-
-    def outer(at):
-        return jnp.where(
-            sub == 7,
-            jnp.broadcast_to(fromnorth_ref[at : at + 1, :], (8, LANES)),
-            jnp.broadcast_to(fromsouth_ref[at : at + 1, :], (8, LANES)),
-        )
-
     edge = (lane < 2) | (lane >= 126)
-
-    def shifts(amount):
-        return (
-            (lane + amount) % LANES,
-            lane < amount,
-            (lane - amount) % LANES,
-            lane >= LANES - amount,
-        )
-
-    def around(x, other, tab):
-        if tab is None:
-            return (
-                roll_lanes(jnp.where(lane == 0, other, x), LANES - 1),
-                roll_lanes(jnp.where(lane == LANES - 1, other, x), 1),
-            )
-        return (
-            pick(jnp.where(tab[1], other, x), tab[0]),
-            pick(jnp.where(tab[3], other, x), tab[2]),
-        )
-
-    def merid_of(t0, t1, t2, last):
-        u0, u1, u2 = (roll_subs(t, 7) for t in (t0, t1, t2))
-        d0, d1, d2 = (roll_subs(t, 1) for t in (t0, t1, t2))
-        bottom = sub == 7
-        top = sub == 0
-        out = [
-            jnp.where(bottom, u1, u0) - jnp.where(top, d2, d0),
-            jnp.where(bottom, u2, u1) - jnp.where(top, d0, d1),
-        ]
-        if last:
-            out.append(jnp.where(bottom, u0, u2) - jnp.where(top, d1, d2))
-        return out
-
-    def take_steps(polar):
+    zero = jnp.zeros((8, LANES), f32)
+
+    def take_step(polar):
         is_polar = (sub < 4) if polar == 0 else (sub >= 4)
 
         def level(k, carry):
@@ -287,29 +300,14 @@
             fc = filter_ref[k]
             pol_at = 8 * (k % 8)
             pol_turn = (4 * polar + 8 - 4 * (k // 8)) % 8
-            gn, hn = k % 4, k // 4
-            gp, hp = k % 2, k // 2
-            s_tab = shifts(shift_ref[8 * polar : 8 * polar + 8, :])
-            m_tab = shifts(shift_ref[ROWS + 8 * polar : ROWS + 8 * polar + 8, :])
-            cz = [cz_ref[0:8, :], cz_ref[8:16, :], outer(LAT_ROWS - 4)]
+            tabs = tables_of(shift_ref, polar)
+            cz = [cz_ref[0:8, :], cz_ref[8:16, :]]
 
             def gather_tiles(v):
                 group = v // 2
                 back = 126 - (v % 2) * 64 - 4 * k
                 cells = [now_ref[v, k, 0:8, :], now_ref[v, k, 8:16, :]]
                 old = [prev_ref[v, k, 0:8, :], prev_ref[v, k, 8:16, :]]
-                at = pl.multiple_of((v * 4 + gn) * 8, 8)
-                t2 = jnp.where(
-                    sub >= 4,
-                    roll_subs(fromnorth_ref[pl.ds(at, 8), :], (14 - 2 * hn) % 8),
-                    roll_subs(fromsouth_ref[pl.ds(at, 8), :], (8 - 2 * hn) % 8),
-                )
-                at = pl.multiple_of((LAT_NOW + v * 2 + gp) * 8, 8)
-                t2_old = jnp.where(
-                    sub >= 4,
-                    roll_subs(fromnorth_ref[pl.ds(at, 8), :], 7 - hp),
-                    roll_subs(fromsouth_ref[pl.ds(at, 8), :], (8 - hp) % 8),
-                )
                 at = pl.multiple_of(v * 64 + pol_at, 8)
                 te = fromeast_ref[pl.ds(at, 8), :]
                 tw = fromwest_ref[pl.ds(at, 8), :]
@@ -326,39 +324,147 @@
                     halo.append(jnp.where(edge, x, strip) if half == polar else x)
                     x = roll_lanes(pstar_ref[tile + 64 : tile + 72, :], back)
                     halo_old.append(jnp.where(edge, x, strip_old) if half == polar else x)
-                t2_halo = roll_lanes(outer(LAT_ROWS - 8 + group), back)
-                return cells, old, t2, t2_old, halo, halo_old, t2_halo
-
-            def tend(x, other, merid, cu, cv, half):
-                right, left = around(x, other, s_tab if half == polar else None)
-                zonal = right - left
-                if half == polar:
-                    right, left = around(x, other, m_tab)
-                return fc * (right + left - 2.0 * x) - cu * zonal - cv * merid
-
-            def first_step(tile, cu_c, cv_c, cu_h, cv_h):
-                cells, old, t2, t2_old, halo, halo_old, t2_halo = tile
-                md = merid_of(cells[0], cells[1], t2, True)
-                mh = merid_of(halo[0], halo[1], t2_halo, False)
+                return cells, old, halo, halo_old
+
+            def advance(v, tiles, cu_c, cv_c, cu_h, cv_h):
+                cells, old, halo, halo_old = tiles
+                md = merid_of(cells[0], cells[1], zero, zero)
+                mh = merid_of(halo[0], halo[1], zero, zero)
+                for h in range(2):
+                    x, o = cells[h], halo[h]
+                    rows = slice(8 * h, 8 * h + 8)
+                    n = old[h] + tend(x, o, md[h], cu_c[h], cv_c[h], fc, *tabs[h])
+                    new_ref[v, k, rows, :] = n
+                    filtered_ref[v, k, rows, :] = x + 0.1 * (old[h] - 2.0 * x + n)
+                    halo_ref[v, k, rows, :] = halo_old[h] + tend(
+                        o, x, mh[h], cu_h[h], cv_h[h], fc, *tabs[h]
+                    )
+
+            u = gather_tiles(0)
+            w = gather_tiles(1)
+            cu_c = [cz[h] * u[0][h] for h in range(2)]
+            cv_c = [mc * w[0][h] for h in range(2)]
+            cu_h = [cz[h] * u[2][h] for h in range(2)]
+            cv_h = [mc * w[2][h] for h in range(2)]
+            for h in range(2):
+                wind_ref[k, 8 * h : 8 * h + 8, :] = w[2][h]
+            for v in range(VARS):
+                tiles = u if v == 0 else w if v == 1 else gather_tiles(v)
+                advance(v, tiles, cu_c, cv_c, cu_h, cv_h)
+            return carry
+
+        lax.fori_loop(0, LEV, level, 0)
+
+    @pl.when(first == 1)
+    def _():
+        take_step(0)
+
+    @pl.when(first != 1)
+    def _():
+        take_step(1)
+
+
+def main_kernel(
+    first_ref,
+    even_ref,
+    merid_ref,
+    filter_ref,
+    now_ref,
+    new_ref,
+    halo_ref,
+    filtered_ref,
+    wind_ref,
+    froma_ref,
+    fromb_ref,
+    shift_ref,
+    cz_ref,
+    mask_ref,
+    w1_ref,
+    b1_ref,
+    w2_ref,
+    b2_ref,
+    w3_ref,
+    b3_ref,
+    start_ref,
+    prev_out,
+    now_out,
+    outp_ref,
+    outn_ref,
+    feats_ref,
+    h2a_ref,
+    h2b_ref,
+    part_ref,
+    sems,
+    last_sem,
+):
+    lane, sub = iotas()
+    first = first_ref[0]
+    even = even_ref[0] == 1
+    bottom = sub == 7
+    top = sub == 0
+    zero = jnp.zeros((8, LANES), f32)
+    north_half = jnp.where(even, sub, 7 - sub) >= 4
+
+    def outer(at):
+        a = jnp.broadcast_to(froma_ref[at : at + 1, :], (8, LANES))
+        b = jnp.broadcast_to(fromb_ref[at : at + 1, :], (8, LANES))
+        return jnp.where(jnp.where(sub == 7, even_ref[0], 1 - even_ref[0]) == 1, b, a)
+
+    def take_steps(polar):
+        def level(k, carry):
+            mc = merid_ref[k]
+            fc = filter_ref[k]
+            gn, hn = k % 4, k // 4
+            gp, hp = k % 2, k // 2
+            tabs = tables_of(shift_ref, polar)
+            cz = [cz_ref[0:8, :], cz_ref[8:16, :], outer(LAT_ROWS - 4)]
+            up_now, down_now = (14 - 2 * hn) % 8, (8 - 2 * hn) % 8
+            up_old, down_old = 7 - hp, (8 - hp) % 8
+            turn_now = (jnp.where(even, down_now, up_now), jnp.where(even, up_now, down_now))
+            turn_old = (jnp.where(even, down_old, up_old), jnp.where(even, up_old, down_old))
+
+            def outer_tiles(v):
+                back = 126 - (v % 2) * 64 - 4 * k
+                pair = []
+                for at, turn in (
+                    ((v * 4 + gn) * 8, turn_now),
+                    ((LAT_NOW + v * 2 + gp) * 8, turn_old),
+                ):
+                    at = pl.multiple_of(at, 8)
+                    a = roll_subs(froma_ref[pl.ds(at, 8), :], turn[0])
+                    b = roll_subs(fromb_ref[pl.ds(at, 8), :], turn[1])
+                    pair.append(jnp.where(north_half, b, a))
+                return pair[0], pair[1], roll_lanes(outer(LAT_ROWS - 8 + v // 2), back)
+
+            def first_step(v, tiles, cu_2, cv_2, cv_c, cv_h):
+                t2, t2_old, t2_halo = tiles
+                above = jnp.where(top, roll_subs(t2, 1), zero)
+                below = jnp.where(bottom, roll_subs(t2, 7), zero)
+                above_h = jnp.where(top, roll_subs(t2_halo, 1), zero)
+                below_h = jnp.where(bottom, roll_subs(t2_halo, 7), zero)
+                more = [cv_c[0] * above, -(cv_c[1] * below)]
+                more_h = [cv_h[0] * above_h, -(cv_h[1] * below_h)]
                 new = []
                 new_halo = []
                 filtered = []
                 for h in range(2):
-                    x, o = cells[h], halo[h]
-                    n = old[h] + tend(x, o, md[h], cu_c[h], cv_c[h], h)
-                    new.append(n)
-                    filtered.append(x + 0.1 * (old[h] - 2.0 * x + n))
-                    new_halo.append(halo_old[h] + tend(o, x, mh[h], cu_h[h], cv_h[h], h))
-                new_t2 = t2_old + tend(t2, t2_halo, md[2], cu_c[2], cv_c[2], 2)
+                    rows = slice(8 * h, 8 * h + 8)
+                    new.append(new_ref[v, k, rows, :] + more[h])
+                    filtered.append(filtered_ref[v, k, rows, :] + 0.1 * more[h])
+                    new_halo.append(halo_ref[v, k, rows, :] + more_h[h])
+                merid = jnp.where(
+                    bottom, roll_subs(now_ref[v, k, 0:8, :], 7), roll_subs(t2, 7)
+                ) - jnp.where(top, roll_subs(now_ref[v, k, 8:16, :], 1), roll_subs(t2, 1))
+                new_t2 = t2_old + tend(t2, t2_halo, merid, cu_2, cv_2, fc, None, None)
                 return new, new_halo, new_t2, filtered
 
             def second_step(v, stepped, cu, cv):
                 new, new_halo, new_t2, filtered = stepped
-                md = merid_of(new[0], new[1], new_t2, False)
+                md = merid_of(new[0], new[1], roll_subs(new_t2, 1), roll_subs(new_t2, 7))
                 both = []
                 for h in range(2):
                     x = new[h]
-                    n = filtered[h] + tend(x, new_halo[h], md[h], cu[h], cv[h], h)
+                    n = filtered[h] + tend(x, new_halo[h], md[h], cu[h], cv[h], fc, *tabs[h])
                     outn_ref[v, k, 8 * h : 8 * h + 8, :] = n
                     outp_ref[v, k, 8 * h : 8 * h + 8, :] = x + 0.1 * (filtered[h] - 2.0 * x + n)
                     both.append(n)
@@ -367,20 +473,20 @@
                     both, axis=0
                 ).astype(bf16)
 
-            u = gather_tiles(0)
-            w = gather_tiles(1)
-            cu_c = [cz[h] * u[0][h] for h in range(2)] + [cz[2] * u[2]]
-            cv_c = [mc * w[0][h] for h in range(2)] + [mc * w[2]]
-            cu_h = [cz[h] * u[4][h] for h in range(2)]
-            cv_h = [mc * w[4][h] for h in range(2)]
-            stepped_u = first_step(u, cu_c, cv_c, cu_h, cv_h)
-            stepped_w = first_step(w, cu_c, cv_c, cu_h, cv_h)
+            u = outer_tiles(0)
+            w = outer_tiles(1)
+            cu_2 = cz[2] * u[0]
+            cv_2 = mc * w[0]
+            cv_c = [mc * now_ref[1, k, 8 * h : 8 * h + 8, :] for h in range(2)]
+            cv_h = [mc * wind_ref[k, 8 * h : 8 * h + 8, :] for h in range(2)]
+            stepped_u = first_step(0, u, cu_2, cv_2, cv_c, cv_h)
+            stepped_w = first_step(1, w, cu_2, cv_2, cv_c, cv_h)
             cu = [cz[h] * stepped_u[0][h] for h in range(2)]
             cv = [mc * stepped_w[0][h] for h in range(2)]
             second_step(0, stepped_u, cu, cv)
             second_step(1, stepped_w, cu, cv)
             for v in range(2, VARS):
-                second_step(v, first_step(gather_tiles(v), cu_c, cv_c, cu_h, cv_h), cu, cv)
+                second_step(v, first_step(v, outer_tiles(v), cu_2, cv_2, cv_c, cv_h), cu, cv)
             pltpu.make_async_copy(outp_ref.at[:, k], prev_out.at[:, k], sems.at[k, 0]).start()
             pltpu.make_async_copy(outn_ref.at[0:2, k], now_out.at[0:2, k], sems.at[k, 1]).start()
             pltpu.make_async_copy(outn_ref.at[3:7, k], now_out.at[3:7, k], sems.at[k, 2]).start()
@@ -489,16 +595,17 @@
     sunlit_count,
 ):
     first = (lax.axis_index("lat") == 0).astype(jnp.int32).reshape(1)
+    even = (lax.axis_index("lat") % 2 == 0).astype(jnp.int32).reshape(1)
     lon = lax.axis_index("lon").astype(jnp.int32).reshape(1)
 
     lon_shape = jax.ShapeDtypeStruct((LON_ROWS, LANES), f32)
     lat_shape = jax.ShapeDtypeStruct((LAT_ROWS, LANES), f32)
     state = jax.ShapeDtypeStruct(state_now.shape, f32)
-    east, west, north, south = pl.pallas_call(
+    east, west, lata, latb = pl.pallas_call(
         pack_kernel,
         name="pack",
         out_shape=(lon_shape, lon_shape, lat_shape, lat_shape),
-        in_specs=[SMEM, SMEM, HBM, HBM],
+        in_specs=[SMEM, SMEM, SMEM, HBM, HBM],
         out_specs=(VMEM,) * 4,
         scratch_shapes=[
             pltpu.VMEM(state_now.shape, f32),
@@ -506,7 +613,7 @@
             pltpu.SemaphoreType.DMA((2, LEV)),
         ],
         compiler_params=pltpu.CompilerParams(vmem_limit_bytes=16 << 20),
-    )(first, zonal_coef, state_now, state_prev)
+    )(first, even, zonal_coef, state_now, state_prev)
 
     def wide(vector):
         return jnp.broadcast_to(vector[:, None], (vector.shape[0], LANES))
@@ -546,32 +653,28 @@
         ]
         return jnp.where(west_cols, pieces[0], pieces[1])
 
-    north = lax.dynamic_update_slice(north, corners(0, 0), (LAT_ROWS - 8, 0))
-    south = lax.dynamic_update_slice(south, corners(1, 7), (LAT_ROWS - 8, 0))
-    (north, south, shift, cz, mask, w1, w2, w3, b1, b2, b3, start) = lax.optimization_barrier(
-        (north, south, shift, cz, mask, w1, w2, w3, b1, b2, b3, start)
-    )
-    fromnorth = lax.ppermute(south, "lat", [(i, i + 1) for i in range(nlat - 1)])
-    fromsouth = lax.ppermute(north, "lat", [(i + 1, i) for i in range(nlat - 1)])
-
-    prev_out, now_out = pl.pallas_call(
-        main_kernel,
-        name="main",
-        out_shape=(state, state),
-        in_specs=[SMEM] * 3 + [VMEM] * 16,
-        out_specs=(ANY, ANY),
-        scratch_shapes=[
-            pltpu.VMEM(state_now.shape, f32),
-            pltpu.VMEM(state_now.shape, f32),
-            pltpu.VMEM((LEV // 2, VARS * ROWS, 2 * LANES), bf16),
-            pltpu.VMEM((8 * TILES_COLS, LANES), f32),
-            pltpu.VMEM((LEV // 2, HID, 2 * LANES), bf16),
-            pltpu.VMEM((LEV // 2, HID, 2 * LANES), bf16),
-            pltpu.VMEM((LEV, 8, LANES), f32),
-            pltpu.SemaphoreType.DMA((LEV, 3)),
-            pltpu.SemaphoreType.DMA,
-        ],
-        compiler_params=pltpu.CompilerParams(vmem_limit_bytes=36 << 20),
+    north, south = corners(0, 0), corners(1, 7)
+    lata = lax.dynamic_update_slice(lata, jnp.where(even == 1, south, north), (LAT_ROWS - 8, 0))
+    latb = lax.dynamic_update_slice(latb, jnp.where(even == 1, north, south), (LAT_ROWS - 8, 0))
+    (lata, latb, shift, cz, mask, w1, w2, w3, b1, b2, b3, start) = lax.optimization_barrier(
+        (lata, latb, shift, cz, mask, w1, w2, w3, b1, b2, b3, start)
+    )
+    swap_a = [(i, i ^ 1) for i in range(nlat)]
+    swap_b = [(i, i + 1 if i % 2 else i - 1) for i in range(1, nlat - 1)]
+    froma = lax.ppermute(lata, "lat", swap_a)
+    fromb = lax.ppermute(latb, "lat", swap_b)
+
+    new, halo, filtered, wind = pl.pallas_call(
+        step_kernel,
+        name="step",
+        out_shape=(state, state, state, jax.ShapeDtypeStruct((LEV, ROWS, LANES), f32)),
+        in_specs=[SMEM] * 3 + [VMEM] * 6,
+        out_specs=(VMEM,) * 4,
+        scratch_shapes=[pltpu.VMEM((8 * TILES_COLS, LANES), f32)],
+        cost_estimate=pl.CostEstimate(
+            flops=20_000_000, bytes_accessed=24_000_000, transcendentals=0
+        ),
+        compiler_params=pltpu.CompilerParams(vmem_limit_bytes=STEPLIM << 20),
     )(
         first,
         merid_coef,
@@ -580,8 +683,39 @@
         state_prev,
         fromwest,
         fromeast,
-        fromnorth,
-        fromsouth,
+        shift,
+        cz,
+    )
+
+    prev_out, now_out = pl.pallas_call(
+        main_kernel,
+        name="main",
+        out_shape=(state, state),
+        in_specs=[SMEM] * 4 + [VMEM] * 17,
+        out_specs=(ANY, ANY),
+        scratch_shapes=[
+            pltpu.VMEM(state_now.shape, f32),
+            pltpu.VMEM(state_now.shape, f32),
+            pltpu.VMEM((LEV // 2, VARS * ROWS, 2 * LANES), bf16),
+            pltpu.VMEM((LEV // 2, HID, 2 * LANES), bf16),
+            pltpu.VMEM((LEV // 2, HID, 2 * LANES), bf16),
+            pltpu.VMEM((LEV, 8, LANES), f32),
+            pltpu.SemaphoreType.DMA((LEV, 3)),
+            pltpu.SemaphoreType.DMA,
+        ],
+        compiler_params=pltpu.CompilerParams(vmem_limit_bytes=MAINLIM << 20),
+    )(
+        first,
+        even,
+        merid_coef,
+        filter_coef,
+        state_now,
+        new,
+        halo,
+        filtered,
+        wind,
+        froma,
+        fromb,
         shift,
         cz,
         mask,

time: 67.4 us -> 64.1 us (0.951)
  the two profiles are of different devices: /device:TPU:63 before, /device:TPU:64 now
where the time goes in v3:
time: 64.1 us; the launch traced here: 63.7 us
  Pallas kernels  34.7 us (54%)
  starting transfers between devices  21.4 us (33%)
  local copies, waits for them, and re-layouts  5.03 us (8%)
  waiting for transfers between devices  1.48 us (2%)
  between operations  1.01 us (2%)
    pallas_call x1, Pallas kernels, body(): pl.pallas_call(main_kernel, name='main', out_shape=(state, state), in_spe...  24.1 us
    ppermute x1, starting transfers between devices, body(): froma = lax.ppermute(lata, 'lat', swap_a)  10.6 us
    pallas_call x1, Pallas kernels, body(): pl.pallas_call(step_kernel, name='step', out_shape=(state, state, state,...  7.06 us
    ppermute x1, starting transfers between devices, body(): lax.ppermute(west, 'lon', [((i + 1) % nlon, i) for i in range(nlon)])  7.01 us
    unnamed x38, local copies, waits for them, and re-layouts  4.61 us
    pallas_call x1, Pallas kernels, body(): pl.pallas_call(pack_kernel, name='pack', out_shape=(lon_shape, lon_shape,...  2.72 us
    ppermute x1, starting transfers between devices, body(): lax.ppermute(east, 'lon', [(i, (i + 1) % nlon) for i in range(nlon)])  1.92 us
    ppermute x1, starting transfers between devices, body(): fromb = lax.ppermute(latb, 'lat', swap_b)  1.92 us
  transfers between devices with their start and end apart: 4, of which 1 were waited for; matrix products, arithmetic and copies ran while one was open for 1% of the time, Pallas kernels for 12%

profile of v3, /device:TPU:64, one launch (start us, length us, event | category | flops | bytes accessed | tf_op | source)
XLA Modules:
  0.0 63.7 jit_solution(13205295157681519008)
XLA Ops:
  0.7 0.6 %copy-done.7 = f32[16]{0:T(128)S(1)} copy-done((f32[16]{0:T(128)S(1)}, f32[16]{0:T(128)}, u32[]{:S(2)}) %copy-start.7) | copy-done | bytes 88
  1.3 1.2 %copy-done = f32[7,16,16,128]{3,2,1,0:T(8,128)S(1)} copy-done((f32[7,16,16,128]{3,2,1,0:T(8,128)S(1)}, f32[7,16,16,128]{3,2,1,0:T(8,128)}, u32[]{:S(2)}) %copy-start) | copy-done | bytes 917528
  2.5 1.2 %copy-done.2 = f32[7,16,16,128]{3,2,1,0:T(8,128)S(1)} copy-done((f32[7,16,16,128]{3,2,1,0:T(8,128)S(1)}, f32[7,16,16,128]{3,2,1,0:T(8,128)}, u32[]{:S(2)}) %copy-start.2) | copy-done | bytes 917528
  3.7 2.7 %pack.1 = (f32[576,128]{1,0:T(8,128)S(1)}, f32[576,128]{1,0:T(8,128)S(1)}, f32[344,128]{1,0:T(8,128)S(1)}, f32[344,128]{1,0:T(8,128)S(1)}) custom-call(s32[1]{0:T(128)} %bitcast.first_ref, s32[1]{0:T(128)} %bitcast.1.even_ref, f32[16]{0:T(128)S(1)} %copy-done.7, f32[7,16,16,128]{3,2,1,0:T(8,128)S(1)} %copy-done, f32[7,16,16,128]{3,2,1,0:T(8,128)S(1)} %copy-done.2), custom_call_target="tpu_custom_call" | custom-call | tf_op jit(solution)/shard_map/pack/pallas_call | solution.py:604
  6.4 0.0 copy-start.12
  6.4 1.9 %collective-permute-start = (f32[576,128]{1,0:T(8,128)S(1)}, f32[576,128]{1,0:T(8,128)S(1)}, u32[]{:S(2)}, u32[]{:S(2)}) collective-permute-start(f32[576,128]{1,0:T(8,128)S(1)} %get-tuple-element.26), channel_id=1, source_target_pairs={{0,12},{12,24},{24,36},{36,48},{48,60},{60,72},{72,84},{84,96},{96... | collective-permute-start | bytes 884744 | tf_op jit(solution)/shard_map/ppermute | solution.py:644
  8.4 7.0 %collective-permute-start.1 = (f32[576,128]{1,0:T(8,128)S(1)}, f32[576,128]{1,0:T(8,128)S(1)}, u32[]{:S(2)}, u32[]{:S(2)}) collective-permute-start(f32[576,128]{1,0:T(8,128)S(1)} %get-tuple-element.27), channel_id=1, source_target_pairs={{12,0},{24,12},{36,24},{48,36},{60,48},{72,60},{84,72},{96,84},{10... | collective-permute-start | bytes 884744 | tf_op jit(solution)/shard_map/ppermute | solution.py:645
  15.5 0.1 copy.26
  15.6 0.0 copy-start.11
  15.6 0.1 copy.25.w1_ref
  15.7 0.7 %copy-done.11 = bf16[64,224]{1,0:T(8,128)(2,1)S(1)} copy-done((bf16[64,224]{1,0:T(8,128)(2,1)S(1)}, bf16[64,224]{1,0:T(8,128)(2,1)}, u32[]{:S(2)}) %copy-start.11) | copy-done | bytes 28696
  16.4 0.1 copy.27
  16.5 0.0 copy-start.8
  16.5 0.0 copy-start.9
  16.5 0.0 copy-start.10
  16.5 0.5 copy-done.4
  17.1 0.1 copy-done.8
  17.2 0.0 copy-done.9
  17.2 0.0 copy-done.10
  17.2 0.9 %prep.1 = (s32[32,128]{1,0:T(8,128)S(1)}, f32[16,128]{1,0:T(8,128)S(1)}, f32[16,128]{1,0:T(8,128)S(1)}, bf16[16,64,112]{2,1,0:T(8,128)(2,1)S(1)}) custom-call(s32[1]{0:T(128)} %bitcast.11.lon_ref, s32[16]{0:T(128)S(1)} %copy-done.8, s32[16]{0:T(128)S(1)} %copy-done.9, f32[16]{0:T(128)S(1)} %copy-done.7, s32[1,64]{1,0:T(1,128)S(1)} %copy-done.10, ...), custom_call_target="tpu_custom_call" | custom-call | tf_op jit(solution)/shard_map/prep/pallas_call | solution.py:622
  18.1 0.0 collective-permute-done.fromwest_ref
  18.1 1.5 %collective-permute-done.1.fromeast_ref = f32[576,128]{1,0:T(8,128)S(1)} collective-permute-done((f32[576,128]{1,0:T(8,128)S(1)}, f32[576,128]{1,0:T(8,128)S(1)}, u32[]{:S(2)}, u32[]{:S(2)}) %collective-permute-start.1) | collective-permute-done | bytes 294944 | tf_op jit(solution)/shard_map/ppermute | solution.py:645
  19.6 0.1 broadcast_in_dim.56.b2_ref
  19.7 0.1 broadcast_in_dim.55.b1_ref
  19.8 0.1 broadcast_in_dim.58.start_ref
  19.9 0.1 broadcast_in_dim.57.b3_ref
  20.0 0.0 copy-start.5
  20.0 0.0 copy-start.6
  20.0 10.6 %collective-permute-start.2 = (f32[344,128]{1,0:T(8,128)S(1)}, f32[344,128]{1,0:T(8,128)S(1)}, u32[]{:S(2)}, u32[]{:S(2)}) collective-permute-start(f32[344,128]{1,0:T(8,128)S(1)} %get-tuple-element.40), channel_id=1, source_target_pairs={{0,1},{1,0},{2,3},{3,2},{4,5},{5,4},{6,7},{7,6},{8,9},{9,8},{10,11... | collective-permute-start | bytes 528392 | tf_op jit(solution)/shard_map/ppermute | solution.py:664
  30.6 1.9 %collective-permute-start.3 = (f32[344,128]{1,0:T(8,128)S(1)}, f32[344,128]{1,0:T(8,128)S(1)}, u32[]{:S(2)}, u32[]{:S(2)}) collective-permute-start(f32[344,128]{1,0:T(8,128)S(1)} %get-tuple-element.41), channel_id=1, source_target_pairs={{1,2},{2,1},{3,4},{4,3},{5,6},{6,5},{7,8},{8,7},{9,10},{10,9},{13,... | collective-permute-start | bytes 528392 | tf_op jit(solution)/shard_map/ppermute | solution.py:665
  32.6 7.1 %step.1 = (f32[7,16,16,128]{3,2,1,0:T(8,128)S(1)}, f32[7,16,16,128]{3,2,1,0:T(8,128)S(1)}, f32[7,16,16,128]{3,2,1,0:T(8,128)S(1)}, f32[16,16,128]{2,1,0:T(8,128)S(1)}) custom-call(s32[1]{0:T(128)} %bitcast.first_ref, f32[16]{0:T(128)S(1)} %copy-done.5, f32[16]{0:T(128)S(1)} %copy-done.6, f32[7,16,16,128]{3,2,1,0:T(8,128)S(1)} %copy-done.1, ...), custom_call_target="tpu_custom_call" | custom-call | flops 20000000 | bytes 24000000 | tf_op jit(solution)/shard_map/step/pallas_call | solution.py:667
  39.6 24.1 %main.1 = (f32[7,16,16,128]{3,2,1,0:T(8,128)}, f32[7,16,16,128]{3,2,1,0:T(8,128)}) custom-call(s32[1]{0:T(128)} %bitcast.first_ref, s32[1]{0:T(128)} %bitcast.1.even_ref, f32[16]{0:T(128)S(1)} %copy-done.5, f32[16]{0:T(128)S(1)} %copy-done.6, f32[7,16,16,128]{3,2,1,0:T(8,128)S(1)} %copy-done.1, f32[7,16,16,128]{3,2,1,0:T(8,128)S(1)} %get-tuple-element.36.new_ref, ...), custom_call_target="tpu_custom_call" | custom-call | tf_op jit(solution)/shard_map/main/pallas_call | solution.py:690
  (38 shorter events, 0.1 us)
Async XLA Ops:
  0.7 0.7 %copy-start.7 = (f32[16]{0:T(128)S(1)}, f32[16]{0:T(128)}, u32[]{:S(2)}) copy-start(f32[16]{0:T(128)} %zc_ref.3) | copy-start | bytes 196
  1.3 1.2 %copy-start = (f32[7,16,16,128]{3,2,1,0:T(8,128)S(1)}, f32[7,16,16,128]{3,2,1,0:T(8,128)}, u32[]{:S(2)}) copy-start(f32[7,16,16,128]{3,2,1,0:T(8,128)} %now_ref.3) | copy-start | bytes 2752516
  2.5 1.2 %copy-start.2 = (f32[7,16,16,128]{3,2,1,0:T(8,128)S(1)}, f32[7,16,16,128]{3,2,1,0:T(8,128)}, u32[]{:S(2)}) copy-start(f32[7,16,16,128]{3,2,1,0:T(8,128)} %prev_ref.1) | copy-start | bytes 2752516
  3.7 11.7 %copy-start.16 = (f32[64]{0:T(128)S(1)}, f32[64]{0:T(128)}, u32[]{:S(2)}) copy-start(f32[64]{0:T(128)} %param.24) | copy-start | bytes 772
  3.7 11.7 %copy-start.14 = (f32[224]{0:T(256)S(1)}, f32[224]{0:T(256)}, u32[]{:S(2)}) copy-start(f32[224]{0:T(256)} %param.28) | copy-start | bytes 2692
  3.7 11.8 %copy-start.15 = (f32[224]{0:T(256)S(1)}, f32[224]{0:T(256)}, u32[]{:S(2)}) copy-start(f32[224]{0:T(256)} %param.29) | copy-start | bytes 2692
  3.7 11.8 %copy-start.13 = (bf16[7,64]{1,0:T(8,128)(2,1)S(1)}, bf16[7,64]{1,0:T(8,128)(2,1)}, u32[]{:S(2)}) copy-start(bf16[7,64]{1,0:T(8,128)(2,1)} %param.23) | copy-start | bytes 2692
  3.7 28.8 %copy-start.1 = (f32[7,16,16,128]{3,2,1,0:T(8,128)S(1)}, f32[7,16,16,128]{3,2,1,0:T(8,128)}, u32[]{:S(2)}) copy-start(f32[7,16,16,128]{3,2,1,0:T(8,128)} %now_ref.3) | copy-start | bytes 2752516
  3.7 28.8 %copy-start.3 = (f32[7,16,16,128]{3,2,1,0:T(8,128)S(1)}, f32[7,16,16,128]{3,2,1,0:T(8,128)}, u32[]{:S(2)}) copy-start(f32[7,16,16,128]{3,2,1,0:T(8,128)} %prev_ref.1) | copy-start | bytes 2752516
  6.4 9.1 %copy-start.12 = (bf16[64,64]{1,0:T(8,128)(2,1)S(1)}, bf16[64,64]{1,0:T(8,128)(2,1)}, u32[]{:S(2)}) copy-start(bf16[64,64]{1,0:T(8,128)(2,1)} %param.25) | copy-start | bytes 24580
  6.4 11.6 %collective-permute-start = (f32[576,128]{1,0:T(8,128)S(1)}, f32[576,128]{1,0:T(8,128)S(1)}, u32[]{:S(2)}, u32[]{:S(2)}) collective-permute-start(f32[576,128]{1,0:T(8,128)S(1)} %get-tuple-element.26), channel_id=1, source_target_pairs={{0,12},{12,24},{24,36},{36,48},{48,60},{60,72},{72,84},{84,96},{96... | collective-permute-start | bytes 884744 | tf_op jit(solution)/shard_map/ppermute | solution.py:644
  8.4 11.2 %collective-permute-start.1 = (f32[576,128]{1,0:T(8,128)S(1)}, f32[576,128]{1,0:T(8,128)S(1)}, u32[]{:S(2)}, u32[]{:S(2)}) collective-permute-start(f32[576,128]{1,0:T(8,128)S(1)} %get-tuple-element.27), channel_id=1, source_target_pairs={{12,0},{24,12},{36,24},{48,36},{60,48},{72,60},{84,72},{96,84},{10... | collective-permute-start | bytes 884744 | tf_op jit(solution)/shard_map/ppermute | solution.py:645
  15.6 0.8 %copy-start.11 = (bf16[64,224]{1,0:T(8,128)(2,1)S(1)}, bf16[64,224]{1,0:T(8,128)(2,1)}, u32[]{:S(2)}) copy-start(bf16[64,224]{1,0:T(8,128)(2,1)} %param.27) | copy-start | bytes 86020
  16.4 0.7 %copy-start.4 = (s32[1,1,1536]{2,1,0:T(1,128)S(1)}, s32[1,1,1536]{2,1,0:T(1,128)}, u32[]{:S(2)}) copy-start(s32[1,1,1536]{2,1,0:T(1,128)} %param.30) | copy-start | bytes 18436
  16.5 0.7 %copy-start.8 = (s32[16]{0:T(128)S(1)}, s32[16]{0:T(128)}, u32[]{:S(2)}) copy-start(s32[16]{0:T(128)} %stride_ref.1) | copy-start | bytes 196
  16.5 0.7 %copy-start.9 = (s32[16]{0:T(128)S(1)}, s32[16]{0:T(128)}, u32[]{:S(2)}) copy-start(s32[16]{0:T(128)} %flen_ref.1) | copy-start | bytes 196
  16.5 0.7 %copy-start.10 = (s32[1,64]{1,0:T(1,128)S(1)}, s32[1,64]{1,0:T(1,128)}, u32[]{:S(2)}) copy-start(s32[1,64]{1,0:T(1,128)} %count_ref.1) | copy-start | bytes 772
  17.2 0.9 %copy-start.17 = (f32[64]{0:T(128)S(1)}, f32[64]{0:T(128)}, u32[]{:S(2)}) copy-start(f32[64]{0:T(128)} %param.26) | copy-start | bytes 772
  20.0 12.6 %copy-start.5 = (f32[16]{0:T(128)S(1)}, f32[16]{0:T(128)}, u32[]{:S(2)}) copy-start(f32[16]{0:T(128)} %merid_ref.3) | copy-start | bytes 196
  20.0 12.5 %copy-start.6 = (f32[16]{0:T(128)S(1)}, f32[16]{0:T(128)}, u32[]{:S(2)}) copy-start(f32[16]{0:T(128)} %filter_ref.3) | copy-start | bytes 196
  20.0 19.6 %collective-permute-start.2 = (f32[344,128]{1,0:T(8,128)S(1)}, f32[344,128]{1,0:T(8,128)S(1)}, u32[]{:S(2)}, u32[]{:S(2)}) collective-permute-start(f32[344,128]{1,0:T(8,128)S(1)} %get-tuple-element.40), channel_id=1, source_target_pairs={{0,1},{1,0},{2,3},{3,2},{4,5},{5,4},{6,7},{7,6},{8,9},{9,8},{10,11... | collective-permute-start | bytes 528392 | tf_op jit(solution)/shard_map/ppermute | solution.py:664
  30.6 9.0 %collective-permute-start.3 = (f32[344,128]{1,0:T(8,128)S(1)}, f32[344,128]{1,0:T(8,128)S(1)}, u32[]{:S(2)}, u32[]{:S(2)}) collective-permute-start(f32[344,128]{1,0:T(8,128)S(1)} %get-tuple-element.41), channel_id=1, source_target_pairs={{1,2},{2,1},{3,4},{4,3},{5,6},{6,5},{7,8},{8,7},{9,10},{10,9},{13,... | collective-permute-start | bytes 528392 | tf_op jit(solution)/shard_map/ppermute | solution.py:665

commit v4 on v3

--- a/solution.py
+++ b/solution.py
@@ -58,7 +58,6 @@
 def pack_kernel(
     first_ref,
     even_ref,
-    zc_ref,
     now_hbm,
     prev_hbm,
     east_ref,
@@ -170,11 +169,6 @@
         return carry
 
     lax.fori_loop(0, 2, rows_prev, 0)
-    put(
-        LAT_ROWS - 8,
-        jnp.full((8, LANES), zc_ref[0], f32),
-        jnp.full((8, LANES), zc_ref[ROWS - 1], f32),
-    )
 
 
 def prep_kernel(
@@ -189,6 +183,7 @@
     cz_out,
     mask_out,
     w1_out,
+    zc_out,
 ):
     sub = lax.broadcasted_iota(jnp.int32, (ROWS, LANES), 0)
     tables = []
@@ -200,6 +195,8 @@
     shift_out[0:ROWS, :] = tables[0]
     shift_out[ROWS : 2 * ROWS, :] = tables[1]
     cz_out[...] = tables[2] * (1.0 / tables[0].astype(f32))
+    zc_out[0:8, :] = jnp.broadcast_to(tables[2][0:1, :], (8, LANES))
+    zc_out[8:16, :] = jnp.broadcast_to(tables[2][15:16, :], (8, LANES))
 
     listed = listed_ref[...]
     live = lax.broadcasted_iota(jnp.int32, (1, LISTED), 1) < count_ref[0, lon_ref[0]]
@@ -605,7 +602,7 @@
         pack_kernel,
         name="pack",
         out_shape=(lon_shape, lon_shape, lat_shape, lat_shape),
-        in_specs=[SMEM, SMEM, SMEM, HBM, HBM],
+        in_specs=[SMEM, SMEM, HBM, HBM],
         out_specs=(VMEM,) * 4,
         scratch_shapes=[
             pltpu.VMEM(state_now.shape, f32),
@@ -613,13 +610,18 @@
             pltpu.SemaphoreType.DMA((2, LEV)),
         ],
         compiler_params=pltpu.CompilerParams(vmem_limit_bytes=16 << 20),
-    )(first, even, zonal_coef, state_now, state_prev)
+    )(
+        first,
+        even,
+        pltpu.with_memory_space_constraint(state_now, pltpu.HBM),
+        pltpu.with_memory_space_constraint(state_prev, pltpu.HBM),
+    )
 
     def wide(vector):
         return jnp.broadcast_to(vector[:, None], (vector.shape[0], LANES))
 
     w1 = jnp.repeat(w_first.T.astype(f32) * 0.5, ROWS, axis=1)
-    shift, cz, mask, w1 = pl.pallas_call(
+    shift, cz, mask, w1, ends = pl.pallas_call(
         prep_kernel,
         name="prep",
         out_shape=(
@@ -627,9 +629,10 @@
             jax.ShapeDtypeStruct((ROWS, LANES), f32),
             jax.ShapeDtypeStruct((ROWS, LANES), f32),
             jax.ShapeDtypeStruct((ROWS, HID, VARS * ROWS), bf16),
+            jax.ShapeDtypeStruct((ROWS, LANES), f32),
         ),
         in_specs=[SMEM] * 5 + [VMEM] * 2,
-        out_specs=(VMEM,) * 4,
+        out_specs=(VMEM,) * 5,
         compiler_params=pltpu.CompilerParams(vmem_limit_bytes=8 << 20),
     )(lon, stride_table, filter_len, zonal_coef, sunlit_count, sunlit_cols.reshape(1, LISTED), w1)
     w2 = (w_second.T.astype(f32) * 0.5).astype(bf16)
@@ -653,6 +656,9 @@
         ]
         return jnp.where(west_cols, pieces[0], pieces[1])
 
+    tail = (LAT_ROWS - 8, 0)
+    lata = lax.dynamic_update_slice(lata, jnp.where(even == 1, ends[8:], ends[:8]), tail)
+    latb = lax.dynamic_update_slice(latb, jnp.where(even == 1, ends[:8], ends[8:]), tail)
     north, south = corners(0, 0), corners(1, 7)
     lata = lax.dynamic_update_slice(lata, jnp.where(even == 1, south, north), (LAT_ROWS - 8, 0))
     latb = lax.dynamic_update_slice(latb, jnp.where(even == 1, north, south), (LAT_ROWS - 8, 0))

time: 64.1 us -> 61.1 us (0.953)
  local copies, waits for them, and re-layouts: 5.03 us -> 2.67 us
    unnamed x38 -> x34, local copies, waits for them, and re-layouts: 4.61 us -> 2.25 us
  transfers between devices with their start and end apart: 4 -> 4, of which waited for: 1 -> 1; matrix products, arithmetic and copies ran while one was open for 1% -> 1% of each run, Pallas kernels for 12% -> 13%
where the time goes in v4:
time: 61.1 us; the launch traced here: 60.8 us
  Pallas kernels  34.8 us (57%)
  starting transfers between devices  21.4 us (35%)
  local copies, waits for them, and re-layouts  2.67 us (4%)
  between operations  1.02 us (2%)
  waiting for transfers between devices  0.85 us (1%)
    pallas_call x1, Pallas kernels, body(): pl.pallas_call(main_kernel, name='main', out_shape=(state, state), in_spe...  24.1 us
    ppermute x1, starting transfers between devices, body(): froma = lax.ppermute(lata, 'lat', swap_a)  10.6 us
    pallas_call x1, Pallas kernels, body(): pl.pallas_call(step_kernel, name='step', out_shape=(state, state, state,...  7.06 us
    ppermute x1, starting transfers between devices, body(): lax.ppermute(west, 'lon', [((i + 1) % nlon, i) for i in range(nlon)])  7.01 us
    pallas_call x1, Pallas kernels, body(): pl.pallas_call(pack_kernel, name='pack', out_shape=(lon_shape, lon_shape,...  2.78 us
    unnamed x34, local copies, waits for them, and re-layouts  2.25 us
    ppermute x1, starting transfers between devices, body(): lax.ppermute(east, 'lon', [(i, (i + 1) % nlon) for i in range(nlon)])  1.92 us
    ppermute x1, starting transfers between devices, body(): fromb = lax.ppermute(latb, 'lat', swap_b)  1.92 us
  transfers between devices with their start and end apart: 4, of which 1 were waited for; matrix products, arithmetic and copies ran while one was open for 1% of the time, Pallas kernels for 13%

profile of v4, /device:TPU:64, one launch (start us, length us, event | category | flops | bytes accessed | tf_op | source)
XLA Modules:
  0.0 60.8 jit_solution(13189026775598227229)
XLA Ops:
  0.7 2.8 %pack.1 = (f32[576,128]{1,0:T(8,128)S(1)}, f32[576,128]{1,0:T(8,128)S(1)}, f32[344,128]{1,0:T(8,128)S(1)}, f32[344,128]{1,0:T(8,128)S(1)}) custom-call(s32[1]{0:T(128)} %bitcast.first_ref, s32[1]{0:T(128)} %bitcast.1.even_ref, f32[7,16,16,128]{3,2,1,0:T(8,128)} %now_ref.3, f32[7,16,16,128]{3,2,1,0:T(8,128)} %prev_ref.1), custom_call_target="tpu_custom_call" | custom-call | tf_op jit(solution)/shard_map/pack/pallas_call | solution.py:601
  3.5 0.0 copy-start.10
  3.5 1.9 %collective-permute-start = (f32[576,128]{1,0:T(8,128)S(1)}, f32[576,128]{1,0:T(8,128)S(1)}, u32[]{:S(2)}, u32[]{:S(2)}) collective-permute-start(f32[576,128]{1,0:T(8,128)S(1)} %get-tuple-element.27), channel_id=1, source_target_pairs={{0,12},{12,24},{24,36},{36,48},{48,60},{60,72},{72,84},{84,96},{96... | collective-permute-start | bytes 884744 | tf_op jit(solution)/shard_map/ppermute | solution.py:647
  5.4 7.0 %collective-permute-start.1 = (f32[576,128]{1,0:T(8,128)S(1)}, f32[576,128]{1,0:T(8,128)S(1)}, u32[]{:S(2)}, u32[]{:S(2)}) collective-permute-start(f32[576,128]{1,0:T(8,128)S(1)} %get-tuple-element.28), channel_id=1, source_target_pairs={{12,0},{24,12},{36,24},{48,36},{60,48},{72,60},{84,72},{96,84},{10... | collective-permute-start | bytes 884744 | tf_op jit(solution)/shard_map/ppermute | solution.py:648
  12.6 0.1 copy.26
  12.7 0.0 copy-start.9
  12.7 0.1 copy.21.w1_ref
  12.8 0.7 %copy-done.9 = bf16[64,224]{1,0:T(8,128)(2,1)S(1)} copy-done((bf16[64,224]{1,0:T(8,128)(2,1)S(1)}, bf16[64,224]{1,0:T(8,128)(2,1)}, u32[]{:S(2)}) %copy-start.9) | copy-done | bytes 28696
  13.5 0.1 copy.27
  13.6 0.0 copy-start.5
  13.6 0.0 copy-start.6
  13.6 0.0 copy-start.7
  13.6 0.5 copy-done.2
  14.2 0.1 copy-done.5
  14.2 0.0 copy-done.6
  14.3 0.0 copy-done.7
  14.3 0.9 %prep.1 = (s32[32,128]{1,0:T(8,128)S(1)}, f32[16,128]{1,0:T(8,128)S(1)}, f32[16,128]{1,0:T(8,128)S(1)}, bf16[16,64,112]{2,1,0:T(8,128)(2,1)S(1)}, f32[16,128]{1,0:T(8,128)S(1)}) custom-call(s32[1]{0:T(128)} %bitcast.3.lon_ref, s32[16]{0:T(128)S(1)} %copy-done.5, s32[16]{0:T(128)S(1)} %copy-done.6, f32[16]{0:T(128)S(1)} %copy-done.7, s32[1,64]{1,0:T(1,128)S(1)} %copy-done.8, ...), custom_call_target="tpu_custom_call" | custom-call | tf_op jit(solution)/shard_map/prep/pallas_call | solution.py:624
  15.2 0.6 %copy-done.15 = f32[64]{0:T(128)S(1)} copy-done((f32[64]{0:T(128)S(1)}, f32[64]{0:T(128)}, u32[]{:S(2)}) %copy-start.15) | copy-done | bytes 280
  15.8 0.0 collective-permute-done.fromwest_ref
  15.8 0.8 %collective-permute-done.1.fromeast_ref = f32[576,128]{1,0:T(8,128)S(1)} collective-permute-done((f32[576,128]{1,0:T(8,128)S(1)}, f32[576,128]{1,0:T(8,128)S(1)}, u32[]{:S(2)}, u32[]{:S(2)}) %collective-permute-start.1) | collective-permute-done | bytes 294944 | tf_op jit(solution)/shard_map/ppermute | solution.py:648
  16.7 0.1 broadcast_in_dim.68.b2_ref
  16.8 0.1 broadcast_in_dim.67.b1_ref
  16.9 0.1 broadcast_in_dim.70.start_ref
  17.0 0.1 broadcast_in_dim.69.b3_ref
  17.1 0.0 copy-start.3
  17.1 0.0 copy-start.4
  17.1 10.6 %collective-permute-start.2 = (f32[344,128]{1,0:T(8,128)S(1)}, f32[344,128]{1,0:T(8,128)S(1)}, u32[]{:S(2)}, u32[]{:S(2)}) collective-permute-start(f32[344,128]{1,0:T(8,128)S(1)} %get-tuple-element.42), channel_id=1, source_target_pairs={{0,1},{1,0},{2,3},{3,2},{4,5},{5,4},{6,7},{7,6},{8,9},{9,8},{10,11... | collective-permute-start | bytes 528392 | tf_op jit(solution)/shard_map/ppermute | solution.py:670
  27.7 1.9 %collective-permute-start.3 = (f32[344,128]{1,0:T(8,128)S(1)}, f32[344,128]{1,0:T(8,128)S(1)}, u32[]{:S(2)}, u32[]{:S(2)}) collective-permute-start(f32[344,128]{1,0:T(8,128)S(1)} %get-tuple-element.43), channel_id=1, source_target_pairs={{1,2},{2,1},{3,4},{4,3},{5,6},{6,5},{7,8},{8,7},{9,10},{10,9},{13,... | collective-permute-start | bytes 528392 | tf_op jit(solution)/shard_map/ppermute | solution.py:671
  29.6 7.1 %step.1 = (f32[7,16,16,128]{3,2,1,0:T(8,128)S(1)}, f32[7,16,16,128]{3,2,1,0:T(8,128)S(1)}, f32[7,16,16,128]{3,2,1,0:T(8,128)S(1)}, f32[16,16,128]{2,1,0:T(8,128)S(1)}) custom-call(s32[1]{0:T(128)} %bitcast.first_ref, f32[16]{0:T(128)S(1)} %copy-done.3, f32[16]{0:T(128)S(1)} %copy-done.4, f32[7,16,16,128]{3,2,1,0:T(8,128)S(1)} %copy-done, ...), custom_call_target="tpu_custom_call" | custom-call | flops 20000000 | bytes 24000000 | tf_op jit(solution)/shard_map/step/pallas_call | solution.py:673
  36.7 0.0 collective-permute-done.2.froma_ref
  36.7 0.0 collective-permute-done.3.fromb_ref
  36.7 24.1 %main.1 = (f32[7,16,16,128]{3,2,1,0:T(8,128)}, f32[7,16,16,128]{3,2,1,0:T(8,128)}) custom-call(s32[1]{0:T(128)} %bitcast.first_ref, s32[1]{0:T(128)} %bitcast.1.even_ref, f32[16]{0:T(128)S(1)} %copy-done.3, f32[16]{0:T(128)S(1)} %copy-done.4, f32[7,16,16,128]{3,2,1,0:T(8,128)S(1)} %copy-done, f32[7,16,16,128]{3,2,1,0:T(8,128)S(1)} %get-tuple-element.38.new_ref, ...), custom_call_target="tpu_custom_call" | custom-call | tf_op jit(solution)/shard_map/main/pallas_call | solution.py:696
  (35 shorter events, 0.1 us)
Async XLA Ops:
  0.7 11.8 %copy-start.14 = (f32[64]{0:T(128)S(1)}, f32[64]{0:T(128)}, u32[]{:S(2)}) copy-start(f32[64]{0:T(128)} %param.24) | copy-start | bytes 772
  0.7 11.8 %copy-start.12 = (f32[224]{0:T(256)S(1)}, f32[224]{0:T(256)}, u32[]{:S(2)}) copy-start(f32[224]{0:T(256)} %param.28) | copy-start | bytes 2692
  0.7 11.8 %copy-start.13 = (f32[224]{0:T(256)S(1)}, f32[224]{0:T(256)}, u32[]{:S(2)}) copy-start(f32[224]{0:T(256)} %param.29) | copy-start | bytes 2692
  0.7 11.9 %copy-start.11 = (bf16[7,64]{1,0:T(8,128)(2,1)S(1)}, bf16[7,64]{1,0:T(8,128)(2,1)}, u32[]{:S(2)}) copy-start(bf16[7,64]{1,0:T(8,128)(2,1)} %param.23) | copy-start | bytes 2692
  0.7 28.9 %copy-start = (f32[7,16,16,128]{3,2,1,0:T(8,128)S(1)}, f32[7,16,16,128]{3,2,1,0:T(8,128)}, u32[]{:S(2)}) copy-start(f32[7,16,16,128]{3,2,1,0:T(8,128)} %now_ref.3) | copy-start | bytes 2752516
  0.7 28.9 %copy-start.1 = (f32[7,16,16,128]{3,2,1,0:T(8,128)S(1)}, f32[7,16,16,128]{3,2,1,0:T(8,128)}, u32[]{:S(2)}) copy-start(f32[7,16,16,128]{3,2,1,0:T(8,128)} %prev_ref.1) | copy-start | bytes 2752516
  3.5 9.1 %copy-start.10 = (bf16[64,64]{1,0:T(8,128)(2,1)S(1)}, bf16[64,64]{1,0:T(8,128)(2,1)}, u32[]{:S(2)}) copy-start(bf16[64,64]{1,0:T(8,128)(2,1)} %param.25) | copy-start | bytes 24580
  3.5 12.3 %collective-permute-start = (f32[576,128]{1,0:T(8,128)S(1)}, f32[576,128]{1,0:T(8,128)S(1)}, u32[]{:S(2)}, u32[]{:S(2)}) collective-permute-start(f32[576,128]{1,0:T(8,128)S(1)} %get-tuple-element.27), channel_id=1, source_target_pairs={{0,12},{12,24},{24,36},{36,48},{48,60},{60,72},{72,84},{84,96},{96... | collective-permute-start | bytes 884744 | tf_op jit(solution)/shard_map/ppermute | solution.py:647
  5.4 11.2 %collective-permute-start.1 = (f32[576,128]{1,0:T(8,128)S(1)}, f32[576,128]{1,0:T(8,128)S(1)}, u32[]{:S(2)}, u32[]{:S(2)}) collective-permute-start(f32[576,128]{1,0:T(8,128)S(1)} %get-tuple-element.28), channel_id=1, source_target_pairs={{12,0},{24,12},{36,24},{48,36},{60,48},{72,60},{84,72},{96,84},{10... | collective-permute-start | bytes 884744 | tf_op jit(solution)/shard_map/ppermute | solution.py:648
  12.7 0.8 %copy-start.9 = (bf16[64,224]{1,0:T(8,128)(2,1)S(1)}, bf16[64,224]{1,0:T(8,128)(2,1)}, u32[]{:S(2)}) copy-start(bf16[64,224]{1,0:T(8,128)(2,1)} %param.27) | copy-start | bytes 86020
  13.5 0.7 %copy-start.2 = (s32[1,1,1536]{2,1,0:T(1,128)S(1)}, s32[1,1,1536]{2,1,0:T(1,128)}, u32[]{:S(2)}) copy-start(s32[1,1,1536]{2,1,0:T(1,128)} %param.30) | copy-start | bytes 18436
  13.5 0.7 %copy-start.8 = (s32[1,64]{1,0:T(1,128)S(1)}, s32[1,64]{1,0:T(1,128)}, u32[]{:S(2)}) copy-start(s32[1,64]{1,0:T(1,128)} %count_ref.1) | copy-start | bytes 772
  13.6 0.7 %copy-start.5 = (s32[16]{0:T(128)S(1)}, s32[16]{0:T(128)}, u32[]{:S(2)}) copy-start(s32[16]{0:T(128)} %stride_ref.1) | copy-start | bytes 196
  13.6 0.7 %copy-start.6 = (s32[16]{0:T(128)S(1)}, s32[16]{0:T(128)}, u32[]{:S(2)}) copy-start(s32[16]{0:T(128)} %flen_ref.1) | copy-start | bytes 196
  13.6 0.7 %copy-start.7 = (f32[16]{0:T(128)S(1)}, f32[16]{0:T(128)}, u32[]{:S(2)}) copy-start(f32[16]{0:T(128)} %zc_ref.1) | copy-start | bytes 196
  15.1 0.7 %copy-start.15 = (f32[64]{0:T(128)S(1)}, f32[64]{0:T(128)}, u32[]{:S(2)}) copy-start(f32[64]{0:T(128)} %param.26) | copy-start | bytes 772
  17.1 12.6 %copy-start.3 = (f32[16]{0:T(128)S(1)}, f32[16]{0:T(128)}, u32[]{:S(2)}) copy-start(f32[16]{0:T(128)} %merid_ref.3) | copy-start | bytes 196
  17.1 12.5 %copy-start.4 = (f32[16]{0:T(128)S(1)}, f32[16]{0:T(128)}, u32[]{:S(2)}) copy-start(f32[16]{0:T(128)} %filter_ref.3) | copy-start | bytes 196
  17.1 19.6 %collective-permute-start.2 = (f32[344,128]{1,0:T(8,128)S(1)}, f32[344,128]{1,0:T(8,128)S(1)}, u32[]{:S(2)}, u32[]{:S(2)}) collective-permute-start(f32[344,128]{1,0:T(8,128)S(1)} %get-tuple-element.42), channel_id=1, source_target_pairs={{0,1},{1,0},{2,3},{3,2},{4,5},{5,4},{6,7},{7,6},{8,9},{9,8},{10,11... | collective-permute-start | bytes 528392 | tf_op jit(solution)/shard_map/ppermute | solution.py:670
  27.7 9.0 %collective-permute-start.3 = (f32[344,128]{1,0:T(8,128)S(1)}, f32[344,128]{1,0:T(8,128)S(1)}, u32[]{:S(2)}, u32[]{:S(2)}) collective-permute-start(f32[344,128]{1,0:T(8,128)S(1)} %get-tuple-element.43), channel_id=1, source_target_pairs={{1,2},{2,1},{3,4},{4,3},{5,6},{6,5},{7,8},{8,7},{9,10},{10,9},{13,... | collective-permute-start | bytes 528392 | tf_op jit(solution)/shard_map/ppermute | solution.py:671
